TPU v7x, 256 devices: a whole 4x4x8 slice. The times are simulated.
256 devices in a mesh: pair: 8 (over y, x_lo), tm: 32 (over x_hi, z, core).
Axes of the slice: x: 4 (x_hi: 2, x_lo: 2; x = x_hi * 2 + x_lo), y: 4, z: 8, core: 2. Of those that a mesh axis runs over, the one named last changes fastest.
Arguments:
- records: bfloat16 [4, 512, 65536], P(None, 'pair', 'tm'), may hold values from -6 to 6
- tile_blocks: int32 [2], replicated, may hold values from 0 to 3, as said below
- live_len: int32 [32], replicated, may hold values from 256 to 512, as said below
Outputs:
- correlations: float32 [512, 512, 801], P('pair', 'tm')
Inputs may be any that keep to these rules, and one draw needn't show every extreme that they name: `live_len`: some segment has exactly 512 live samples. `tile_blocks`: the two blocks differ, and one of them is block 3.
All inputs are finite; a program needn't handle non-finite values.
Results may differ from a plain program's by a relative error of at most 0.0036.
Values may be sent and summed in bfloat16 or wider, within the bound.
A program may use at most 384 MiB of HBM per device.

v0:
```python
import functools
import math

import jax
import jax.numpy as jnp
import ml_dtypes
import numpy as np
from jax import lax
from jax.experimental import pallas as pl
from jax.experimental.pallas import tpu as pltpu
from jax.sharding import PartitionSpec as P

DECIM = 4
TAPS = 64
SEG = 512
NFT = 1024
MAXLAG = 400
SMOOTH = 4
BINS = 512
LAGS = 801
LANE = 128
QUARTERS = 4
CHUNKS = 4
KCHUNK = LANE // CHUNKS
TWO_PI = 2.0 * math.pi / NFT
F32 = jnp.float32
BF16 = jnp.bfloat16


def split_np(table):
    high = table.astype(ml_dtypes.bfloat16)
    low = (table - high.astype(np.float64)).astype(ml_dtypes.bfloat16)
    return high, low


def filter_table():
    index = np.arange(TAPS, dtype=np.float64)
    centred = (index - (TAPS - 1) / 2.0) / DECIM
    window = 0.5 * (1.0 - np.cos(2.0 * np.pi * (index + 0.5) / TAPS))
    taps = window * np.sin(np.pi * centred) / (np.pi * centred) / DECIM
    table = np.zeros((5 * LANE, LANE))
    for j in range(LANE):
        table[TAPS + DECIM * j : 2 * TAPS + DECIM * j, j] = taps
    high, low = split_np(table)
    return np.concatenate([high, low], axis=1)


def turn_tables():
    sample = np.arange(SEG)
    coarse = (8 * np.arange(BINS // 8))[:, None] * sample[None, :] % NFT
    fine = np.arange(8)[:, None] * sample[None, :] % NFT
    pick = lambda fn, phase: fn(phase * TWO_PI).astype(np.float32)
    return (
        pick(np.cos, coarse),
        pick(np.sin, coarse),
        pick(np.cos, fine),
        pick(np.sin, fine),
    )


def bin_order():
    chunk = np.arange(CHUNKS)[:, None, None]
    quarter = np.arange(QUARTERS)[None, :, None]
    inner = np.arange(KCHUNK)[None, None, :]
    return (quarter * LANE + chunk * KCHUNK + inner).reshape(-1)


def lag_table():
    bins = bin_order()
    shifts = np.arange(LAGS) - MAXLAG
    phase = (bins[:, None] * shifts[None, :] % NFT) * TWO_PI
    weights = np.where(bins == 0, 1.0, 2.0)[:, None] / math.sqrt(NFT)
    table = np.concatenate([weights * np.cos(phase), -weights * np.sin(phase)], axis=0)
    return table.astype(ml_dtypes.bfloat16)


def split(value):
    high = value.astype(BF16)
    return high, (value - high.astype(F32)).astype(BF16)


def dot(a, b, dims=((1,), (0,))):
    return lax.dot_general(a, b, (dims, ((), ())), preferred_element_type=F32)


def prepare_kernel(
    blocks, live, row_ref, col_ref, row_tail, col_tail, taps_ref,
    coarse_cos, coarse_sin, fine_cos, fine_sin,
    row_out, col_out, fwd_high, fwd_low, padded,
):
    del blocks
    fc, fs = fine_cos[...], fine_sin[...]
    for a in range(BINS // 8):
        cc = coarse_cos[a : a + 1, :]
        cs = coarse_sin[a : a + 1, :]
        rows = slice(8 * a, 8 * a + 8)
        for value, base in ((cc * fc - cs * fs, 0), (-(cs * fc + cc * fs), BINS)):
            high, low = split(value)
            fwd_high[base + rows.start : base + rows.stop, :] = high
            fwd_low[base + rows.start : base + rows.stop, :] = low

    record = jnp.concatenate([row_ref[0], col_ref[0]], axis=0)
    tail = jnp.concatenate([row_tail[0], col_tail[0]], axis=0)
    count = live[0]
    lane = lax.broadcasted_iota(jnp.int32, (1, LANE), 1)
    pieces = []
    for b in range(SEG // LANE):
        span = DECIM * LANE
        before = tail if b == 0 else record[:, b * span - LANE : b * span]
        both = dot(before, taps_ref[:LANE, :]) + dot(
            record[:, b * span : (b + 1) * span], taps_ref[LANE:, :]
        )
        value = both[:, :LANE] + both[:, LANE:]
        pieces.append(jnp.where(lane + b * LANE < count, value, 0.0))
    filtered = jnp.concatenate(pieces, axis=1)
    high, low = split(filtered)
    last = ((1,), (1,))
    spectra = (
        dot(fwd_high[...], low, last)
        + dot(fwd_low[...], high, last)
        + dot(fwd_high[...], high, last)
    )
    real, imag = spectra[:BINS], spectra[BINS:]
    amplitude = jnp.sqrt(real * real + imag * imag)
    padded[0:8, :] = jnp.zeros((8, LANE), F32)
    padded[8 + BINS : 16 + BINS, :] = jnp.zeros((8, LANE), F32)
    padded[8 : 8 + BINS, :] = amplitude
    smooth = padded[8 - SMOOTH : 8 - SMOOTH + BINS, :]
    for offset in range(1, 2 * SMOOTH + 1):
        start = 8 - SMOOTH + offset
        smooth = smooth + padded[start : start + BINS, :]
    mean = jnp.sum(amplitude, axis=0, keepdims=True) * (1.0 / BINS)
    level = smooth * (1.0 / (2 * SMOOTH + 1)) + 0.05 * mean + 1e-06
    inverse = 1.0 / level
    real = real * inverse
    imag = imag * inverse
    half = LANE // 2
    lower = lax.broadcasted_iota(jnp.int32, (BINS, LANE), 1) < half
    row_out[...] = jnp.where(lower, real, pltpu.roll(imag, half, 1)).astype(BF16)
    cols = jnp.where(lower, pltpu.roll(real, half, 1), imag)
    lanes = lax.broadcasted_iota(jnp.int32, (LANE, LANE), 1)
    for j in range(4):
        total = jnp.zeros((LANE, LANE), F32)
        for quarter in range(QUARTERS):
            part = cols[quarter * LANE : (quarter + 1) * LANE, :]
            for c in range(2):
                source = c * half + 16 * j
                target = quarter * 32 + 16 * c
                moved = part
                if (target - source) % LANE:
                    moved = pltpu.roll(part, (target - source) % LANE, 1)
                keep = (lanes >= target) & (lanes < target + 16)
                total = jnp.where(keep, moved, total)
        col_out[j] = total.astype(BF16)


def prepare(records, tails, tile_blocks, live):
    stations, length = records.shape[1], records.shape[2]
    whole = lambda *shape: pl.BlockSpec(shape, lambda i, b, l: (0,) * len(shape))
    taps = jnp.asarray(filter_table())
    tables = [jnp.asarray(table) for table in turn_tables()]
    return pl.pallas_call(
        prepare_kernel,
        grid_spec=pltpu.PrefetchScalarGridSpec(
            num_scalar_prefetch=2,
            grid=(1,),
            in_specs=[
                pl.BlockSpec((1, stations, length), lambda i, b, l: (b[0], 0, 0)),
                pl.BlockSpec((1, stations, length), lambda i, b, l: (b[1], 0, 0)),
                pl.BlockSpec((1, stations, LANE), lambda i, b, l: (b[0], 0, 0)),
                pl.BlockSpec((1, stations, LANE), lambda i, b, l: (b[1], 0, 0)),
                whole(5 * LANE, 2 * LANE),
                whole(BINS // 8, SEG),
                whole(BINS // 8, SEG),
                whole(8, SEG),
                whole(8, SEG),
            ],
            out_specs=[whole(BINS, LANE), whole(4, LANE, LANE)],
            scratch_shapes=[
                pltpu.VMEM((2 * BINS, SEG), BF16),
                pltpu.VMEM((2 * BINS, SEG), BF16),
                pltpu.VMEM((BINS + 16, LANE), F32),
            ],
        ),
        out_shape=[
            jax.ShapeDtypeStruct((BINS, LANE), BF16),
            jax.ShapeDtypeStruct((4, LANE, LANE), BF16),
        ],
        compiler_params=pltpu.CompilerParams(vmem_limit_bytes=40 << 20),
        name="prepare",
    )(tile_blocks, live, records, records, tails, tails, taps, *tables)


def correlate_kernel(segments, row_ref, col_ref, lag_ref, out_ref, rows, cols, cross, stacked):
    step = pl.program_id(0)
    half = LANE // 2
    group = 8
    count_k = QUARTERS * KCHUNK

    @pl.when(step < CHUNKS)
    def _():
        rows[...] = row_ref[...].reshape(segments * count_k, LANE).astype(F32)
        cols[...] = col_ref[...].reshape(segments * KCHUNK, LANE).astype(F32)
        lane = lax.broadcasted_iota(jnp.int32, (32, group * segments), 1)
        sign = jnp.where(
            lax.broadcasted_iota(jnp.int32, (1, LANE), 1) < half, 1.0, -1.0
        ).astype(F32)
        for block in range(KCHUNK // group):
            gathered = jnp.concatenate(
                [
                    cols[pl.ds(block * group + b, segments, stride=KCHUNK), :]
                    for b in range(group)
                ],
                axis=0,
            )
            turned = gathered.T.astype(BF16)
            for quarter in range(QUARTERS):
                left = turned[quarter * 32 : quarter * 32 + 32, :]
                zero = jnp.zeros_like(left)
                wide = jnp.concatenate(
                    [
                        jnp.where(
                            (lane >= b * segments) & (lane < (b + 1) * segments), left, zero
                        )
                        for b in range(group)
                    ],
                    axis=0,
                )
                base = quarter * KCHUNK + block * group
                right = jnp.concatenate(
                    [
                        rows[pl.ds(base + b, segments, stride=count_k), :]
                        for b in range(group)
                    ],
                    axis=0,
                ).astype(BF16)
                product = dot(wide, right)
                for b in range(group):
                    top = product[b * 32 : b * 32 + 16, :]
                    low = product[b * 32 + 16 : b * 32 + 32, :]
                    value = top + sign * pltpu.roll(low, half, 1)
                    cross[pl.ds(base + b, 16, stride=count_k), :] = value
        for q in range(16):
            turned = cross[q * count_k : (q + 1) * count_k, :].T.astype(BF16)
            for chunk in range(CHUNKS):

                @pl.when(step == chunk)
                def _():
                    at = chunk * count_k
                    stacked[q * half : (q + 1) * half, at : at + count_k] = turned[:half]
                    stacked[q * half : (q + 1) * half, BINS + at : BINS + at + count_k] = turned[half:]

    @pl.when(step >= CHUNKS)
    def _():
        for q in range(16):
            value = dot(stacked[q * half : (q + 1) * half, :], lag_ref[...])
            out_ref[pl.ds(q, half, stride=16), :] = value


def correlate(row_all, col_all):
    segments = row_all.shape[0]
    row_all = row_all.reshape(segments, QUARTERS, LANE, LANE)
    table = lag_table()
    width = LANE
    tiles = -(-LAGS // width)
    table = jnp.asarray(np.pad(table, ((0, 0), (0, tiles * width - LAGS))))
    pairs = 16 * (LANE // 2)

    body = functools.partial(correlate_kernel, segments)
    return pl.pallas_call(
        body,
        grid=(CHUNKS + tiles,),
        in_specs=[
            pl.BlockSpec(
                (segments, QUARTERS, KCHUNK, LANE),
                lambda i: (0, 0, jnp.minimum(i, CHUNKS - 1), 0),
            ),
            pl.BlockSpec(
                (segments, KCHUNK, LANE), lambda i: (0, jnp.minimum(i, CHUNKS - 1), 0)
            ),
            pl.BlockSpec((2 * BINS, width), lambda i: (0, jnp.maximum(i - CHUNKS, 0))),
        ],
        out_specs=pl.BlockSpec((pairs, width), lambda i: (0, jnp.maximum(i - CHUNKS, 0))),
        out_shape=jax.ShapeDtypeStruct((pairs, LAGS), F32),
        scratch_shapes=[
            pltpu.VMEM((segments * QUARTERS * KCHUNK, LANE), F32),
            pltpu.VMEM((segments * KCHUNK, LANE), F32),
            pltpu.VMEM((16 * QUARTERS * KCHUNK, LANE), F32),
            pltpu.VMEM((pairs, 2 * BINS), BF16),
        ],
        compiler_params=pltpu.CompilerParams(vmem_limit_bytes=48 << 20),
        name="correlate",
    )(row_all, col_all, table)


def shards(records, tile_blocks, live_len):
    length = records.shape[2]
    size = lax.axis_size("tm")
    tails = lax.ppermute(
        records[:, :, length - LANE :], "tm", [(i, i + 1) for i in range(size - 1)]
    )
    live = lax.dynamic_slice(live_len, (lax.axis_index("tm"),), (1,))
    row_own, col_own = prepare(records, tails, tile_blocks, live)
    row_all = lax.all_gather(row_own, "tm", axis=0)
    col_rows = lax.all_gather(col_own, "pair", axis=0, tiled=True)
    col_all = lax.all_to_all(col_rows, "tm", split_axis=0, concat_axis=0, tiled=True)
    result = correlate(row_all, col_all)
    return result.reshape(LANE // 2, 16, LAGS)


def solution(mesh):
    placed = (P(None, "pair", "tm"), P(), P())
    return jax.shard_map(
        shards, mesh=mesh, in_specs=placed, out_specs=P("pair", "tm", None), check_vma=False
    )
```

profile of v0, /device:TPU:14, one launch (start us, length us, event | category | flops | bytes accessed | tf_op | source)
XLA Modules:
  0.0 193.1 jit_solution(9827604559839568749)
XLA Ops:
  6.5 0.0 all-gather.4.cloned.1.call-start
  6.5 0.8 slice.3
  7.4 1.9 collective-permute-start
  9.3 1.3 dynamic_slice.3.live
  10.6 6.8 %collective-permute-done.row_tail.col_tail = bf16[4,64,128]{2,1,0:T(8,128)(2,1)S(1)} collective-permute-done((bf16[4,64,128]{2,1,0:T(8,128)(2,1)S(1)}, bf16[4,64,128]{2,1,0:T(8,128)(2,1)S(1)}, u32[]{:S(2)}, u32[]{:S(2)}) %collective-permute-start) | collective-permute-done | bytes 65568 | tf_op jit(solution)/shard_map/ppermute | solution.py:299
  17.4 0.0 copy-start
  17.4 1.2 copy-done
  18.6 0.0 copy-start.2
  18.6 1.0 copy-done.2
  19.6 0.0 copy-start.3
  19.6 0.9 copy-done.3
  20.5 0.0 copy-start.4
  20.5 0.9 copy-done.4
  21.4 0.0 copy-start.5
  21.4 0.7 copy-done.5
  22.1 0.0 copy-start.6
  22.1 0.7 copy-done.6
  22.8 0.0 copy-start.7
  22.8 0.7 copy-done.7
  23.5 0.0 copy-start.1
  23.5 3.8 %prepare.1 = (bf16[512,128]{1,0:T(8,128)(2,1)}, bf16[4,128,128]{2,1,0:T(8,128)(2,1)}) custom-call(s32[2]{0:T(128)S(1)} %copy-done.7, s32[1]{0:T(128)} %dynamic_slice.3.live, bf16[4,64,2048]{2,1,0:T(8,128)(2,1)S(1)} %copy-done, bf16[4,64,2048]{2,1,0:T(8,128)(2,1)S(1)} %copy-done, bf16[4,64,128]{2,1,0:T(8,128)(2,1)S(1)} %collective-permute-done.row_tail.col_tail, ...), custom_call_target="tpu_custom_call" | custom-call | tf_op jit(solution)/shard_map/prepare/pallas_call | solution.py:162
  27.3 0.0 all-gather.4.cloned.1.call-update
  27.3 0.0 all-gather.6.cloned.1.call-start
  27.4 0.7 all-gather.6.cloned.1.call-update
  28.1 37.9 %all-gather.4.cloned.1.call-done = bf16[32,128,128]{2,1,0:T(8,128)(2,1)} async-done(((bf16[4,128,128]{2,1,0:T(8,128)(2,1)}), bf16[32,128,128]{2,1,0:T(8,128)(2,1)}) %all-gather.4.cloned.1.call-update) | async-done | bytes 1048592 | tf_op jit(solution)/shard_map/all_gather | solution.py:305
  66.0 39.6 %all_to_all.5.col_ref = bf16[32,128,128]{2,1,0:T(8,128)(2,1)S(1)} all-to-all(bf16[32,128,128]{2,1,0:T(8,128)(2,1)} %all-gather.4.cloned.1.call-done), channel_id=1, replica_groups=mesh['pair'=8,'tm'=32] {'tm'}, dimensions={0} | all-to-all | bytes 2097152 | tf_op jit(solution)/shard_map/all_to_all | solution.py:306
  105.6 55.4 %all-gather.6.cloned.1.call-done = bf16[16384,128]{1,0:T(8,128)(2,1)} async-done(((bf16[512,128]{1,0:T(8,128)(2,1)}), bf16[16384,128]{1,0:T(8,128)(2,1)}) %all-gather.6.cloned.1.call-update) | async-done | bytes 4194320 | tf_op jit(solution)/shard_map/all_gather | solution.py:304
  161.0 0.0 copy-done.1
  161.0 25.3 %correlate.1 = f32[1024,801]{1,0:T(8,128)} custom-call(bf16[32,4,128,128]{3,2,1,0:T(8,128)(2,1)} %bitcast.2, bf16[32,128,128]{2,1,0:T(8,128)(2,1)S(1)} %all_to_all.5.col_ref, bf16[1024,896]{1,0:T(8,128)(2,1)S(1)} %copy-done.1), custom_call_target="tpu_custom_call" | custom-call | tf_op jit(solution)/shard_map/correlate/pallas_call | solution.py:270
Async XLA Ops:
  6.5 59.5 %all-gather.4.cloned.1.call-start = ((), (), s32[]{:S(2)}) async-start(), calls=%async_computation.1 | async-start | bytes 1179648 | tf_op jit(solution)/shard_map/all_gather | solution.py:305
  7.4 10.0 %collective-permute-start = (bf16[4,64,128]{2,1,0:T(8,128)(2,1)S(1)}, bf16[4,64,128]{2,1,0:T(8,128)(2,1)S(1)}, u32[]{:S(2)}, u32[]{:S(2)}) collective-permute-start(bf16[4,64,128]{2,1,0:T(8,128)(2,1)S(1)} %slice.3), channel_id=1, source_target_pairs={{0,1},{1,2},{2,3},{3,4},{4,5},{5,6},{6,7},{7,8},{8,9},{9,10},{10,1... | collective-permute-start | bytes 196616 | tf_op jit(solution)/shard_map/ppermute | solution.py:299
  17.4 1.2 copy-start
  18.6 1.0 copy-start.2
  19.6 0.9 copy-start.3
  20.5 0.9 copy-start.4
  21.4 0.7 copy-start.5
  22.1 0.7 copy-start.6
  22.8 0.7 copy-start.7
  23.5 137.6 %copy-start.1 = (bf16[1024,896]{1,0:T(8,128)(2,1)S(1)}, bf16[1024,896]{1,0:T(8,128)(2,1)}, u32[]{:S(2)}) copy-start(bf16[1024,896]{1,0:T(8,128)(2,1)} %constant.25.clone.lag_ref) | copy-start | bytes 5505028
  27.3 133.7 %all-gather.6.cloned.1.call-start = ((), (), s32[]{:S(2)}) async-start(), calls=%async_computation.2 | async-start | bytes 4325376 | tf_op jit(solution)/shard_map/all_gather | solution.py:304
Sparse Core Ops, SparseCore 0:
  27.5 38.5 all-gather.3
  68.8 92.1 all-gather.5
where the time goes:
time: 197 us; the launch traced here: 193 us
  waiting for transfers between devices  101 us (51%)
  blocking collectives  39.6 us (20%)
  Pallas kernels  29.1 us (15%)
  between operations  13.4 us (7%)
  local copies, waits for them, and re-layouts  8.24 us (4%)
    all_gather x1, waiting for transfers between devices, shards(): row_all = lax.all_gather(row_own, 'tm', axis=0)  55.4 us
    all_to_all x1, blocking collectives, shards(): lax.all_to_all(col_rows, 'tm', split_axis=0, concat_axis=0, tiled=True)  39.6 us
    all_gather x1, waiting for transfers between devices, shards(): col_rows = lax.all_gather(col_own, 'pair', axis=0, tiled=True)  37.9 us
    pallas_call x1, Pallas kernels, correlate(): pl.pallas_call(body, grid=(CHUNKS + tiles,), in_specs=[pl.BlockSpec((segm...  25.3 us
    ppermute x1, waiting for transfers between devices, shards(): lax.ppermute(records[:, :, length - LANE:], 'tm', [(i, i + 1) for i in ra...  6.75 us
    unnamed x16, local copies, waits for them, and re-layouts  6.1 us
  transfers between devices with their start and end apart: 3, of which 3 were waited for; matrix products, arithmetic and copies ran while one was open for 1% of the time, Pallas kernels for 0%

commit v1 on v0

--- a/solution.py
+++ b/solution.py
@@ -25,6 +25,10 @@
 TWO_PI = 2.0 * math.pi / NFT
 F32 = jnp.float32
 BF16 = jnp.bfloat16
+MESH = pl.DeviceIdType.MESH
+RING = 8
+YRING = 4
+OFFSETS = (0, 1, -1, 2, -2, 3, -3, 4)
 
 
 def split_np(table):
@@ -191,6 +195,295 @@
     )(tile_blocks, live, records, records, tails, tails, taps, *tables)
 
 
+class Place:
+    def __init__(self):
+        pair, tm = lax.axis_index("pair"), lax.axis_index("tm")
+        self.y, self.xl = pair // 2, lax.rem(pair, 2)
+        self.xh, self.z, self.c = tm // 16, lax.rem(tm // 2, RING), lax.rem(tm, 2)
+
+    def at(self, y=None, xl=None, xh=None, z=None, c=None):
+        pick = lambda new, old: old if new is None else new
+        y, xl, xh = pick(y, self.y), pick(xl, self.xl), pick(xh, self.xh)
+        z, c = pick(z, self.z), pick(c, self.c)
+        return {"pair": y * 2 + xl, "tm": xh * 16 + z * 2 + c}
+
+
+def slot_of(xh, c, z):
+    return xh * 16 + c * RING + z
+
+
+def schedule():
+    events = []
+    for i, base in enumerate((1.5, 3.5, 3.6, 6.5, 6.6, 9.5, 9.6, 12.5)):
+        events.append((base, "root", i))
+        events.append((base + 2.0, "other", i))
+        events.append((base + 4.0, "near", i))
+        events.append((base + 7.0, "chain", i))
+    for d in range(1, 5):
+        events.append((1.0 + 4.6 * d, "row", (0, d)))
+        events.append((3.0 + 4.6 * d, "row", (1, d)))
+    events.append((2.9, "opposite", None))
+    events.sort(key=lambda e: e[0])
+    return [(kind, arg) for _, kind, arg in events]
+
+
+def exchange_kernel(
+    row_ref, col_ref, row_all, col_all, stage,
+    row_send, row_recv, stage_send, stage_recv, col_send, col_recv, local_sem,
+):
+    me = Place()
+    half_rows = BINS // 2
+    group_xh = me.y // 2
+    home_y = me.xh * 2 + me.z // 4
+    home_xl = lax.rem(me.z // 2, 2)
+    dy = lax.rem(me.y - home_y + YRING, YRING)
+    root_pair = lax.rem(me.y, 2) * 2 + me.xl
+    is_root = (me.z // 2) == root_pair
+    is_near = is_root & (me.xh == group_xh)
+    is_far = is_root & (me.xh != group_xh)
+    is_other = (dy == 0) & (me.xl != home_xl)
+    up, down = lax.rem(me.y + 1, YRING), lax.rem(me.y + YRING - 1, YRING)
+    right, left = lax.rem(me.z + 1, RING), lax.rem(me.z + RING - 1, RING)
+
+    barrier = pltpu.get_barrier_semaphore()
+
+    def greet(device):
+        pl.semaphore_signal(barrier, inc=1, device_id=device, device_id_type=MESH)
+
+    for step in range(1, 2 * RING):
+        other = lax.rem(me.z * 2 + me.c + step, 2 * RING)
+        greet(me.at(z=other // 2, c=lax.rem(other, 2)))
+    greet(me.at(xh=1 - me.xh))
+    greet(me.at(xl=1 - me.xl))
+    greet(me.at(xh=1 - me.xh, xl=1 - me.xl))
+    greet(me.at(y=up))
+    greet(me.at(y=down))
+    pl.semaphore_wait(barrier, 2 * RING - 1 + 5)
+
+    def remote(src, dst, send, recv, device):
+        return pltpu.make_async_remote_copy(
+            src_ref=src, dst_ref=dst, send_sem=send, recv_sem=recv,
+            device_id=device, device_id_type=MESH,
+        )
+
+    pending = []
+
+    def start(copy, when=None):
+        if when is None:
+            copy.start()
+        else:
+            pl.when(when)(copy.start)
+        pending.append((copy, when))
+
+    for j in range(4):
+        root_z, root_c = root_pair * 2 + j // 2, j % 2
+        mine = (me.z == root_z) & (me.c == root_c)
+        index = me.c * RING + me.z
+        copy = remote(
+            col_ref.at[j], stage.at[index], stage_send.at[j], stage_recv.at[index],
+            me.at(z=root_z, c=root_c),
+        )
+        start(copy, jnp.logical_not(mine))
+
+        @pl.when(mine)
+        def _():
+            pltpu.make_async_copy(col_ref.at[j], stage.at[index], stage_recv.at[index]).start()
+
+    own = slot_of(me.xh, me.c, me.z)
+    own_local = pltpu.make_async_copy(row_ref, row_all.at[own], local_sem.at[16])
+    start(
+        remote(row_ref, row_all.at[own], row_send.at[32], row_recv.at[own, 0], me.at(xh=1 - me.xh))
+    )
+
+    def spread(source, slot, h, d, direction):
+        base = h * 16
+        for sign, target, offset in ((1, right, 0), (-1, left, 4)):
+            if direction not in (0, sign) or d > 3:
+                continue
+            send = row_send.at[base + offset + d]
+            device = me.at(z=target)
+            if d < 3:
+                start(remote(source, row_all.at[slot], send, row_recv.at[slot, 0], device))
+            else:
+                part = 0 if sign == 1 else 1
+                rows = pl.ds(part * half_rows, half_rows)
+                start(
+                    remote(
+                        source.at[rows], row_all.at[slot, rows], send,
+                        row_recv.at[slot, part], device,
+                    )
+                )
+        number = 15 if d == 4 else 8 + (d + 3 if direction == -1 else d)
+        start(
+            remote(
+                source, row_all.at[slot], row_send.at[base + number],
+                row_recv.at[slot, 0], me.at(c=1 - me.c),
+            )
+        )
+
+    def got_row(slot, part=None):
+        if part is None:
+            ref = row_all.at[slot]
+        else:
+            ref = row_all.at[slot, pl.ds(part * half_rows, half_rows)]
+        remote(ref, ref, row_send.at[0], row_recv.at[slot, part or 0], me.at()).wait_recv()
+
+    def got_col(slot):
+        ref = col_all.at[slot]
+        remote(ref, ref, col_send.at[0, 0], col_recv.at[slot], me.at()).wait_recv()
+
+    spread(row_ref, own, 0, 0, 0)
+    own_local.start()
+
+    def zpiece(i):
+        return lax.rem(me.z + OFFSETS[i] + RING, RING)
+
+    def along(source, slot, c, when):
+        start(
+            remote(
+                source, col_all.at[slot], col_send.at[slot, 1], col_recv.at[slot],
+                me.at(y=up if c == 0 else down),
+            ),
+            when,
+        )
+
+    for kind, arg in schedule():
+        if kind == "opposite":
+            slot = slot_of(1 - me.xh, me.c, me.z)
+            got_row(slot)
+            spread(row_all.at[slot], slot, 1, 0, 0)
+        elif kind == "row":
+            h, d = arg
+            xh = me.xh if h == 0 else 1 - me.xh
+            if d < 4:
+                for sign in (1, -1):
+                    slot = slot_of(xh, me.c, lax.rem(me.z - sign * d + RING, RING))
+                    got_row(slot)
+                    spread(row_all.at[slot], slot, h, d, sign)
+            else:
+                slot = slot_of(xh, me.c, lax.rem(me.z + 4, RING))
+                got_row(slot, 0)
+                got_row(slot, 1)
+                spread(row_all.at[slot], slot, h, d, 1)
+        elif kind == "root":
+            for c in range(2):
+                index = c * RING + zpiece(arg)
+                slot = slot_of(me.xh, c, zpiece(arg))
+
+                @pl.when(is_root)
+                def _():
+                    pltpu.make_async_copy(
+                        stage.at[index], stage.at[index], stage_recv.at[index]
+                    ).wait()
+
+                @pl.when(is_near)
+                def _():
+                    pltpu.make_async_copy(
+                        stage.at[index], col_all.at[slot], local_sem.at[2 * arg + c]
+                    ).start()
+
+                start(
+                    remote(
+                        stage.at[index], col_all.at[slot], col_send.at[slot, 0],
+                        col_recv.at[slot], me.at(xl=1 - me.xl),
+                    ),
+                    is_near,
+                )
+                start(
+                    remote(
+                        stage.at[index], col_all.at[slot], col_send.at[slot, 0],
+                        col_recv.at[slot], me.at(xl=1 - me.xl, xh=1 - me.xh),
+                    ),
+                    is_far,
+                )
+                along(stage.at[index], slot, c, is_near)
+        elif kind == "other":
+            for far in (0, 1):
+                xh = 1 - me.xh if far else me.xh
+                for c in range(2):
+                    slot = slot_of(xh, c, zpiece(arg))
+                    pl.when(is_other)(lambda slot=slot: got_col(slot))
+                    if far:
+                        start(
+                            remote(
+                                col_all.at[slot], col_all.at[slot], col_send.at[slot, 0],
+                                col_recv.at[slot], me.at(xl=1 - me.xl),
+                            ),
+                            is_other,
+                        )
+                    along(col_all.at[slot], slot, c, is_other)
+        elif kind == "near":
+            for c in range(2):
+                slot = slot_of(1 - me.xh, c, zpiece(arg))
+                pl.when(is_near)(lambda slot=slot: got_col(slot))
+                along(col_all.at[slot], slot, c, is_near)
+        elif kind == "chain":
+            for far in (0, 1):
+                xh = 1 - me.xh if far else me.xh
+                first = slot_of(xh, 0, zpiece(arg))
+                second = slot_of(xh, 1, zpiece(arg))
+
+                @pl.when(dy == 3)
+                def _():
+                    got_col(second)
+
+                along(col_all.at[second], second, 1, dy == 3)
+
+                @pl.when(dy != 0)
+                def _():
+                    got_col(first)
+
+                along(col_all.at[first], first, 0, (dy == 1) | (dy == 2))
+
+                @pl.when((dy == 1) | (dy == 2))
+                def _():
+                    got_col(second)
+
+                along(col_all.at[second], second, 1, dy == 2)
+
+    for h in range(2):
+        for z in range(RING):
+            got_row(slot_of(h, 1 - me.c, z))
+    own_local.wait()
+    for i in range(RING):
+        for c in range(2):
+            index = c * RING + zpiece(i)
+            slot = slot_of(me.xh, c, zpiece(i))
+
+            @pl.when(is_near)
+            def _():
+                pltpu.make_async_copy(
+                    stage.at[index], col_all.at[slot], local_sem.at[2 * i + c]
+                ).wait()
+
+    for copy, when in pending:
+        if when is None:
+            copy.wait_send()
+        else:
+            pl.when(when)(copy.wait_send)
+
+
+def exchange(row_own, col_own):
+    anywhere = pl.BlockSpec(memory_space=pl.ANY)
+    dma = pltpu.SemaphoreType.DMA
+    return pl.pallas_call(
+        exchange_kernel,
+        in_specs=[anywhere, anywhere],
+        out_specs=[anywhere, anywhere],
+        out_shape=[
+            jax.ShapeDtypeStruct((32,) + row_own.shape, BF16),
+            jax.ShapeDtypeStruct((32,) + col_own.shape[1:], BF16),
+        ],
+        scratch_shapes=[
+            pltpu.VMEM((2 * RING,) + col_own.shape[1:], BF16),
+            dma((33,)), dma((32, 2)), dma((4,)), dma((2 * RING,)),
+            dma((32, 2)), dma((32,)), dma((17,)),
+        ],
+        compiler_params=pltpu.CompilerParams(collective_id=0, has_side_effects=True),
+        name="exchange",
+    )(row_own, col_own)
+
+
 def correlate_kernel(segments, row_ref, col_ref, lag_ref, out_ref, rows, cols, cross, stacked):
     step = pl.program_id(0)
     half = LANE // 2
@@ -301,9 +594,7 @@
     )
     live = lax.dynamic_slice(live_len, (lax.axis_index("tm"),), (1,))
     row_own, col_own = prepare(records, tails, tile_blocks, live)
-    row_all = lax.all_gather(row_own, "tm", axis=0)
-    col_rows = lax.all_gather(col_own, "pair", axis=0, tiled=True)
-    col_all = lax.all_to_all(col_rows, "tm", split_axis=0, concat_axis=0, tiled=True)
+    row_all, col_all = exchange(row_own, col_own)
     result = correlate(row_all, col_all)
     return result.reshape(LANE // 2, 16, LAGS)
 

time: 197 us -> 193 us (0.980); the launches traced: 193 us -> 192 us
  Pallas kernels: 29.1 us -> 172 us
  waiting for transfers between devices: 101 us -> 6.81 us
  blocking collectives: 39.6 us -> 0 us
  between operations: 13.4 us -> 0.06 us
  local copies, waits for them, and re-layouts: 8.24 us -> 10.7 us
    pallas_call x0 -> x1, Pallas kernels: none -> 144 us  [exchange(): pl.pallas_call(exchange_kernel, in_specs=[anywhere, anywhere], out_specs=...]
    all_gather x2 -> x0, waiting for transfers between devices: 93.3 us -> none  [the longest x1 55.4 us: shards(): row_all = lax.all_gather(row_own, 'tm', axis=0)]
    all_to_all x1 -> x0, blocking collectives: 39.6 us -> none  [shards(): lax.all_to_all(col_rows, 'tm', split_axis=0, concat_axis=0, tiled=True)]
    unnamed x16 -> x22, local copies, waits for them, and re-layouts: 6.1 us -> 8.62 us
  transfers between devices with their start and end apart: 3 -> 1, of which waited for: 3 -> 1; matrix products, arithmetic and copies ran while one was open for 1% -> 1% of each run, Pallas kernels for 0% -> 0%
where the time goes in v1:
time: 193 us; the launch traced here: 192 us
  Pallas kernels  172 us (89%)
  local copies, waits for them, and re-layouts  10.7 us (6%)
  waiting for transfers between devices  6.81 us (4%)
    pallas_call x1, Pallas kernels, exchange(): pl.pallas_call(exchange_kernel, in_specs=[anywhere, anywhere], out_specs=...  144 us
    pallas_call x1, Pallas kernels, correlate(): pl.pallas_call(body, grid=(CHUNKS + tiles,), in_specs=[pl.BlockSpec((segm...  25.3 us
    unnamed x22, local copies, waits for them, and re-layouts  8.62 us
    ppermute x1, waiting for transfers between devices, shards(): lax.ppermute(records[:, :, length - LANE:], 'tm', [(i, i + 1) for i in ra...  6.81 us
  transfers between devices with their start and end apart: 1, of which 1 were waited for; matrix products, arithmetic and copies ran while one was open for 1% of the time, Pallas kernels for 0%

profile of v1, /device:TPU:14, one launch (start us, length us, event | category | flops | bytes accessed | tf_op | source)
XLA Modules:
  0.0 191.9 jit_solution(13103636370157884147)
XLA Ops:
  0.0 0.8 slice.3
  0.8 1.9 collective-permute-start
  2.8 1.2 dynamic_slice.3.live
  4.0 6.8 %collective-permute-done.row_tail.col_tail = bf16[4,64,128]{2,1,0:T(8,128)(2,1)S(1)} collective-permute-done((bf16[4,64,128]{2,1,0:T(8,128)(2,1)S(1)}, bf16[4,64,128]{2,1,0:T(8,128)(2,1)S(1)}, u32[]{:S(2)}, u32[]{:S(2)}) %collective-permute-start) | collective-permute-done | bytes 65568 | tf_op jit(solution)/shard_map/ppermute | solution.py:592
  10.8 0.0 copy-start
  10.8 1.2 copy-done
  12.0 0.0 copy-start.3
  12.1 1.0 copy-done.3
  13.0 0.0 copy-start.6
  13.0 0.9 copy-done.6
  13.9 0.0 copy-start.7
  13.9 0.9 copy-done.7
  14.8 0.0 copy-start.8
  14.8 0.7 copy-done.8
  15.5 0.0 copy-start.9
  15.6 0.7 copy-done.9
  16.3 0.0 copy-start.10
  16.3 0.7 copy-done.10
  16.9 0.0 copy-start.1
  16.9 3.2 %prepare.1 = (bf16[512,128]{1,0:T(8,128)(2,1)S(1)}, bf16[4,128,128]{2,1,0:T(8,128)(2,1)S(1)}) custom-call(s32[2]{0:T(128)S(1)} %copy-done.10, s32[1]{0:T(128)} %dynamic_slice.3.live, bf16[4,64,2048]{2,1,0:T(8,128)(2,1)S(1)} %copy-done, bf16[4,64,2048]{2,1,0:T(8,128)(2,1)S(1)} %copy-done, bf16[4,64,128]{2,1,0:T(8,128)(2,1)S(1)} %collective-permute-done.row_tail.col_tail, ...), custom_call_target="tpu_custom_call" | custom-call | tf_op jit(solution)/shard_map/prepare/pallas_call | solution.py:166
  20.2 0.0 copy-start.4
  20.2 0.6 copy-done.4
  20.8 0.0 copy-start.5
  20.8 0.7 copy-done.5
  21.5 143.9 %exchange.1 = (bf16[32,512,128]{2,1,0:T(8,128)(2,1)}, bf16[32,128,128]{2,1,0:T(8,128)(2,1)}) custom-call(bf16[512,128]{1,0:T(8,128)(2,1)} %copy-done.4, bf16[4,128,128]{2,1,0:T(8,128)(2,1)} %copy-done.5), custom_call_target="tpu_custom_call" | custom-call | tf_op jit(solution)/shard_map/exchange/pallas_call | solution.py:469
  165.3 0.0 copy-done.1
  165.3 0.0 copy-start.2
  165.4 1.2 copy-done.2
  166.6 25.3 %correlate.1 = f32[1024,801]{1,0:T(8,128)} custom-call(bf16[32,4,128,128]{3,2,1,0:T(8,128)(2,1)} %bitcast.2, bf16[32,128,128]{2,1,0:T(8,128)(2,1)S(1)} %copy-done.2, bf16[1024,896]{1,0:T(8,128)(2,1)S(1)} %copy-done.1), custom_call_target="tpu_custom_call" | custom-call | tf_op jit(solution)/shard_map/correlate/pallas_call | solution.py:563
Async XLA Ops:
  0.8 10.0 %collective-permute-start = (bf16[4,64,128]{2,1,0:T(8,128)(2,1)S(1)}, bf16[4,64,128]{2,1,0:T(8,128)(2,1)S(1)}, u32[]{:S(2)}, u32[]{:S(2)}) collective-permute-start(bf16[4,64,128]{2,1,0:T(8,128)(2,1)S(1)} %slice.3), channel_id=1, source_target_pairs={{0,1},{1,2},{2,3},{3,4},{4,5},{5,6},{6,7},{7,8},{8,9},{9,10},{10,1... | collective-permute-start | bytes 196616 | tf_op jit(solution)/shard_map/ppermute | solution.py:592
  10.8 1.2 copy-start
  12.0 1.0 copy-start.3
  13.0 0.9 copy-start.6
  13.9 0.9 copy-start.7
  14.8 0.7 copy-start.8
  15.5 0.7 copy-start.9
  16.3 0.7 copy-start.10
  16.9 148.4 %copy-start.1 = (bf16[1024,896]{1,0:T(8,128)(2,1)S(1)}, bf16[1024,896]{1,0:T(8,128)(2,1)}, u32[]{:S(2)}) copy-start(bf16[1024,896]{1,0:T(8,128)(2,1)} %constant.25.clone.lag_ref) | copy-start | bytes 5505028
  20.2 0.7 copy-start.4
  20.8 0.7 copy-start.5
  165.3 1.2 copy-start.2

commit v2 on v1

--- a/solution.py
+++ b/solution.py
@@ -29,6 +29,18 @@
 RING = 8
 YRING = 4
 OFFSETS = (0, 1, -1, 2, -2, 3, -3, 4)
+PARTS = 2
+OPP_TIME = 3.0
+ROW_START, ROW_STEP = 5.0, 5.0
+COL_STEP = 1.5
+COL_TIMES = (
+    ("root", 1.5),
+    ("other", 8.0),
+    ("near", 10.5),
+    ("hop1", 13.0),
+    ("hop2", 16.0),
+    ("last", 40.0),
+)
 
 
 def split_np(table):
@@ -214,25 +226,26 @@
 
 def schedule():
     events = []
-    for i, base in enumerate((1.5, 3.5, 3.6, 6.5, 6.6, 9.5, 9.6, 12.5)):
-        events.append((base, "root", i))
-        events.append((base + 2.0, "other", i))
-        events.append((base + 4.0, "near", i))
-        events.append((base + 7.0, "chain", i))
-    for d in range(1, 5):
-        events.append((1.0 + 4.6 * d, "row", (0, d)))
-        events.append((3.0 + 4.6 * d, "row", (1, d)))
-    events.append((2.9, "opposite", None))
+    for i in range(RING):
+        for kind, late in COL_TIMES:
+            events.append((late + COL_STEP * i, kind, i))
+    for s in range(PARTS):
+        events.append((OPP_TIME + 0.1 * s, "opposite", s))
+        for d in range(1, 5):
+            for h in range(2):
+                at = ROW_START + ROW_STEP * (d - 1) + (0.5 * ROW_STEP * h + 0.45 * ROW_STEP * s / PARTS)
+                events.append((at, "row", (h, d, s)))
     events.sort(key=lambda e: e[0])
     return [(kind, arg) for _, kind, arg in events]
 
 
 def exchange_kernel(
     row_ref, col_ref, row_all, col_all, stage,
-    row_send, row_recv, stage_send, stage_recv, col_send, col_recv, local_sem,
+    row_send, row_recv, near_send, near_recv, stage_send, stage_recv,
+    col_send, col_recv, local_sem,
 ):
     me = Place()
-    half_rows = BINS // 2
+    size = BINS // PARTS
     group_xh = me.y // 2
     home_y = me.xh * 2 + me.z // 4
     home_xl = lax.rem(me.z // 2, 2)
@@ -290,49 +303,48 @@
             pltpu.make_async_copy(col_ref.at[j], stage.at[index], stage_recv.at[index]).start()
 
     own = slot_of(me.xh, me.c, me.z)
-    own_local = pltpu.make_async_copy(row_ref, row_all.at[own], local_sem.at[16])
-    start(
-        remote(row_ref, row_all.at[own], row_send.at[32], row_recv.at[own, 0], me.at(xh=1 - me.xh))
-    )
-
-    def spread(source, slot, h, d, direction):
-        base = h * 16
-        for sign, target, offset in ((1, right, 0), (-1, left, 4)):
-            if direction not in (0, sign) or d > 3:
+    own_local = pltpu.make_async_copy(row_ref, row_all.at[own], local_sem.at[2 * RING])
+
+    def part(s):
+        return pl.ds(s * size, size)
+
+    def spread(source, slot, h, d, sign, s):
+        lower = s < PARTS // 2
+        for way, target in ((1, right), (-1, left)):
+            if sign not in (0, way) or d > 3 or (d == 3 and lower != (way == 1)):
                 continue
-            send = row_send.at[base + offset + d]
-            device = me.at(z=target)
-            if d < 3:
-                start(remote(source, row_all.at[slot], send, row_recv.at[slot, 0], device))
-            else:
-                part = 0 if sign == 1 else 1
-                rows = pl.ds(part * half_rows, half_rows)
-                start(
-                    remote(
-                        source.at[rows], row_all.at[slot, rows], send,
-                        row_recv.at[slot, part], device,
-                    )
+            start(
+                remote(
+                    source.at[part(s)], row_all.at[slot, part(s)],
+                    row_send.at[h, (0 if way == 1 else 4) + d, s], row_recv.at[slot, s],
+                    me.at(z=target),
                 )
-        number = 15 if d == 4 else 8 + (d + 3 if direction == -1 else d)
+            )
+        number = d + 3 if sign == -1 and d < 4 else (7 if d == 4 else d)
         start(
             remote(
-                source, row_all.at[slot], row_send.at[base + number],
-                row_recv.at[slot, 0], me.at(c=1 - me.c),
+                source.at[part(s)], row_all.at[slot, part(s)], near_send.at[h, number, s],
+                near_recv.at[slot, s], me.at(c=1 - me.c),
             )
         )
 
-    def got_row(slot, part=None):
-        if part is None:
-            ref = row_all.at[slot]
-        else:
-            ref = row_all.at[slot, pl.ds(part * half_rows, half_rows)]
-        remote(ref, ref, row_send.at[0], row_recv.at[slot, part or 0], me.at()).wait_recv()
+    def got_row(slot, s, sems):
+        ref = row_all.at[slot, part(s)]
+        remote(ref, ref, row_send.at[0, 0, 0], sems.at[slot, s], me.at()).wait_recv()
 
     def got_col(slot):
         ref = col_all.at[slot]
         remote(ref, ref, col_send.at[0, 0], col_recv.at[slot], me.at()).wait_recv()
 
-    spread(row_ref, own, 0, 0, 0)
+    for s in range(PARTS):
+        start(
+            remote(
+                row_ref.at[part(s)], row_all.at[own, part(s)], row_send.at[2, 0, s],
+                row_recv.at[own, s], me.at(xh=1 - me.xh),
+            )
+        )
+    for s in range(PARTS):
+        spread(row_ref, own, 0, 0, 0, s)
     own_local.start()
 
     def zpiece(i):
@@ -347,24 +359,32 @@
             when,
         )
 
+    def sideways(source, slot, when, **there):
+        start(
+            remote(
+                source, col_all.at[slot], col_send.at[slot, 0], col_recv.at[slot],
+                me.at(xl=1 - me.xl, **there),
+            ),
+            when,
+        )
+
+    def hop(slot, c, when):
+        pl.when(when)(lambda: got_col(slot))
+        along(col_all.at[slot], slot, c, when)
+
     for kind, arg in schedule():
         if kind == "opposite":
             slot = slot_of(1 - me.xh, me.c, me.z)
-            got_row(slot)
-            spread(row_all.at[slot], slot, 1, 0, 0)
+            got_row(slot, arg, row_recv)
+            spread(row_all.at[slot], slot, 1, 0, 0, arg)
         elif kind == "row":
-            h, d = arg
+            h, d, s = arg
             xh = me.xh if h == 0 else 1 - me.xh
-            if d < 4:
-                for sign in (1, -1):
-                    slot = slot_of(xh, me.c, lax.rem(me.z - sign * d + RING, RING))
-                    got_row(slot)
-                    spread(row_all.at[slot], slot, h, d, sign)
-            else:
-                slot = slot_of(xh, me.c, lax.rem(me.z + 4, RING))
-                got_row(slot, 0)
-                got_row(slot, 1)
-                spread(row_all.at[slot], slot, h, d, 1)
+            signs = (1, -1) if d < 4 else ((1,) if s < PARTS // 2 else (-1,))
+            for sign in signs:
+                slot = slot_of(xh, me.c, lax.rem(me.z - sign * d + RING, RING))
+                got_row(slot, s, row_recv)
+                spread(row_all.at[slot], slot, h, d, sign, s)
         elif kind == "root":
             for c in range(2):
                 index = c * RING + zpiece(arg)
@@ -382,68 +402,37 @@
                         stage.at[index], col_all.at[slot], local_sem.at[2 * arg + c]
                     ).start()
 
-                start(
-                    remote(
-                        stage.at[index], col_all.at[slot], col_send.at[slot, 0],
-                        col_recv.at[slot], me.at(xl=1 - me.xl),
-                    ),
-                    is_near,
-                )
-                start(
-                    remote(
-                        stage.at[index], col_all.at[slot], col_send.at[slot, 0],
-                        col_recv.at[slot], me.at(xl=1 - me.xl, xh=1 - me.xh),
-                    ),
-                    is_far,
-                )
+                sideways(stage.at[index], slot, is_near)
+                sideways(stage.at[index], slot, is_far, xh=1 - me.xh)
                 along(stage.at[index], slot, c, is_near)
         elif kind == "other":
-            for far in (0, 1):
-                xh = 1 - me.xh if far else me.xh
-                for c in range(2):
-                    slot = slot_of(xh, c, zpiece(arg))
-                    pl.when(is_other)(lambda slot=slot: got_col(slot))
-                    if far:
-                        start(
-                            remote(
-                                col_all.at[slot], col_all.at[slot], col_send.at[slot, 0],
-                                col_recv.at[slot], me.at(xl=1 - me.xl),
-                            ),
-                            is_other,
-                        )
-                    along(col_all.at[slot], slot, c, is_other)
+            for c in range(2):
+                slot = slot_of(1 - me.xh, c, zpiece(arg))
+                pl.when(is_other)(lambda slot=slot: got_col(slot))
+                sideways(col_all.at[slot], slot, is_other)
+                along(col_all.at[slot], slot, c, is_other)
+            for c in range(2):
+                hop(slot_of(me.xh, c, zpiece(arg)), c, is_other)
         elif kind == "near":
             for c in range(2):
-                slot = slot_of(1 - me.xh, c, zpiece(arg))
-                pl.when(is_near)(lambda slot=slot: got_col(slot))
-                along(col_all.at[slot], slot, c, is_near)
-        elif kind == "chain":
-            for far in (0, 1):
-                xh = 1 - me.xh if far else me.xh
-                first = slot_of(xh, 0, zpiece(arg))
-                second = slot_of(xh, 1, zpiece(arg))
-
-                @pl.when(dy == 3)
-                def _():
-                    got_col(second)
-
-                along(col_all.at[second], second, 1, dy == 3)
-
-                @pl.when(dy != 0)
-                def _():
-                    got_col(first)
-
-                along(col_all.at[first], first, 0, (dy == 1) | (dy == 2))
-
-                @pl.when((dy == 1) | (dy == 2))
-                def _():
-                    got_col(second)
-
-                along(col_all.at[second], second, 1, dy == 2)
+                hop(slot_of(1 - me.xh, c, zpiece(arg)), c, is_near)
+        elif kind == "hop1":
+            for xh in (me.xh, 1 - me.xh):
+                hop(slot_of(xh, 0, zpiece(arg)), 0, dy == 1)
+                hop(slot_of(xh, 1, zpiece(arg)), 1, dy == 3)
+        elif kind == "hop2":
+            for xh in (me.xh, 1 - me.xh):
+                for c in range(2):
+                    hop(slot_of(xh, c, zpiece(arg)), c, dy == 2)
+        elif kind == "last":
+            for xh in (me.xh, 1 - me.xh):
+                pl.when(dy == 3)(lambda xh=xh: got_col(slot_of(xh, 0, zpiece(arg))))
+                pl.when(dy == 1)(lambda xh=xh: got_col(slot_of(xh, 1, zpiece(arg))))
 
     for h in range(2):
         for z in range(RING):
-            got_row(slot_of(h, 1 - me.c, z))
+            for s in range(PARTS):
+                got_row(slot_of(h, 1 - me.c, z), s, near_recv)
     own_local.wait()
     for i in range(RING):
         for c in range(2):
@@ -476,8 +465,8 @@
         ],
         scratch_shapes=[
             pltpu.VMEM((2 * RING,) + col_own.shape[1:], BF16),
-            dma((33,)), dma((32, 2)), dma((4,)), dma((2 * RING,)),
-            dma((32, 2)), dma((32,)), dma((17,)),
+            dma((3, 8, PARTS)), dma((32, PARTS)), dma((2, 8, PARTS)), dma((32, PARTS)),
+            dma((4,)), dma((2 * RING,)), dma((32, 2)), dma((32,)), dma((2 * RING + 1,)),
         ],
         compiler_params=pltpu.CompilerParams(collective_id=0, has_side_effects=True),
         name="exchange",

time: 193 us -> 96.5 us (0.50)
  Pallas kernels: 172 us -> 76.5 us
    pallas_call x1, Pallas kernels: 144 us -> 48 us  [exchange(): pl.pallas_call(exchange_kernel, in_specs=[anywhere, anywhere], out_specs=...]
where the time goes in v2:
time: 96.5 us; the launch traced here: 96 us
  Pallas kernels  76.5 us (79%)
  local copies, waits for them, and re-layouts  10.7 us (11%)
  waiting for transfers between devices  6.81 us (7%)
  starting transfers between devices  1.91 us (2%)
    pallas_call x1, Pallas kernels, exchange(): pl.pallas_call(exchange_kernel, in_specs=[anywhere, anywhere], out_specs=...  48 us
    pallas_call x1, Pallas kernels, correlate(): pl.pallas_call(body, grid=(CHUNKS + tiles,), in_specs=[pl.BlockSpec((segm...  25.3 us
    unnamed x22, local copies, waits for them, and re-layouts  8.62 us
    ppermute x1, waiting for transfers between devices, shards(): lax.ppermute(records[:, :, length - LANE:], 'tm', [(i, i + 1) for i in ra...  6.81 us
    pallas_call x1, Pallas kernels, prepare(): pl.pallas_call(prepare_kernel, grid_spec=pltpu.PrefetchScalarGridSpec(num...  3.22 us
  transfers between devices with their start and end apart: 1, of which 1 were waited for; matrix products, arithmetic and copies ran while one was open for 1% of the time, Pallas kernels for 0%

profile of v2, /device:TPU:14, one launch (start us, length us, event | category | flops | bytes accessed | tf_op | source)
XLA Modules:
  0.0 96.0 jit_solution(4721324870679065259)
XLA Ops:
  0.0 0.8 slice.3
  0.8 1.9 %collective-permute-start = (bf16[4,64,128]{2,1,0:T(8,128)(2,1)S(1)}, bf16[4,64,128]{2,1,0:T(8,128)(2,1)S(1)}, u32[]{:S(2)}, u32[]{:S(2)}) collective-permute-start(bf16[4,64,128]{2,1,0:T(8,128)(2,1)S(1)} %slice.3), channel_id=1, source_target_pairs={{0,1},{1,2},{2,3},{3,4},{4,5},{5,6},{6,7},{7,8},{8,9},{9,10},{10,1... | collective-permute-start | bytes 196616 | tf_op jit(solution)/shard_map/ppermute | solution.py:581
  2.8 1.2 %dynamic_slice.3.live = s32[1]{0:T(128)} dynamic-slice(s32[32]{0:T(128)} %param.11, s32[]{:T(128)S(6)} %select_n.3), dynamic_slice_sizes={1} | dynamic-slice | bytes 12 | tf_op jit(solution)/shard_map/dynamic_slice | solution.py:584
  4.0 6.8 %collective-permute-done.row_tail.col_tail = bf16[4,64,128]{2,1,0:T(8,128)(2,1)S(1)} collective-permute-done((bf16[4,64,128]{2,1,0:T(8,128)(2,1)S(1)}, bf16[4,64,128]{2,1,0:T(8,128)(2,1)S(1)}, u32[]{:S(2)}, u32[]{:S(2)}) %collective-permute-start) | collective-permute-done | bytes 65568 | tf_op jit(solution)/shard_map/ppermute | solution.py:581
  10.8 0.0 copy-start
  10.8 1.2 %copy-done = bf16[4,64,2048]{2,1,0:T(8,128)(2,1)S(1)} copy-done((bf16[4,64,2048]{2,1,0:T(8,128)(2,1)S(1)}, bf16[4,64,2048]{2,1,0:T(8,128)(2,1)}, u32[]{:S(2)}) %copy-start) | copy-done | bytes 1048600
  12.0 0.0 copy-start.3
  12.1 1.0 %copy-done.3 = bf16[640,256]{1,0:T(8,128)(2,1)S(1)} copy-done((bf16[640,256]{1,0:T(8,128)(2,1)S(1)}, bf16[640,256]{1,0:T(8,128)(2,1)}, u32[]{:S(2)}) %copy-start.3) | copy-done | bytes 327704
  13.0 0.0 copy-start.6
  13.0 0.9 copy-done.6
  13.9 0.0 copy-start.7
  13.9 0.9 copy-done.7
  14.8 0.0 copy-start.8
  14.8 0.7 copy-done.8
  15.5 0.0 copy-start.9
  15.6 0.7 copy-done.9
  16.3 0.0 copy-start.10
  16.3 0.7 copy-done.10
  16.9 0.0 copy-start.1
  16.9 3.2 %prepare.1 = (bf16[512,128]{1,0:T(8,128)(2,1)S(1)}, bf16[4,128,128]{2,1,0:T(8,128)(2,1)S(1)}) custom-call(s32[2]{0:T(128)S(1)} %copy-done.10, s32[1]{0:T(128)} %dynamic_slice.3.live, bf16[4,64,2048]{2,1,0:T(8,128)(2,1)S(1)} %copy-done, bf16[4,64,2048]{2,1,0:T(8,128)(2,1)S(1)} %copy-done, bf16[4,64,128]{2,1,0:T(8,128)(2,1)S(1)} %collective-permute-done.row_tail.col_tail, ...), custom_call_target="tpu_custom_call" | custom-call | tf_op jit(solution)/shard_map/prepare/pallas_call | solution.py:178
  20.2 0.0 copy-start.4
  20.2 0.6 copy-done.4
  20.8 0.0 copy-start.5
  20.8 0.7 copy-done.5
  21.5 48.0 %exchange.1 = (bf16[32,512,128]{2,1,0:T(8,128)(2,1)}, bf16[32,128,128]{2,1,0:T(8,128)(2,1)}) custom-call(bf16[512,128]{1,0:T(8,128)(2,1)} %copy-done.4, bf16[4,128,128]{2,1,0:T(8,128)(2,1)} %copy-done.5), custom_call_target="tpu_custom_call" | custom-call | tf_op jit(solution)/shard_map/exchange/pallas_call | solution.py:458
  69.4 0.0 copy-done.1
  69.5 0.0 copy-start.2
  69.5 1.2 %copy-done.2 = bf16[32,128,128]{2,1,0:T(8,128)(2,1)S(1)} copy-done((bf16[32,128,128]{2,1,0:T(8,128)(2,1)S(1)}, bf16[32,128,128]{2,1,0:T(8,128)(2,1)}, u32[]{:S(2)}) %copy-start.2) | copy-done | bytes 1048600
  70.7 25.3 %correlate.1 = f32[1024,801]{1,0:T(8,128)} custom-call(bf16[32,4,128,128]{3,2,1,0:T(8,128)(2,1)} %bitcast.2, bf16[32,128,128]{2,1,0:T(8,128)(2,1)S(1)} %copy-done.2, bf16[1024,896]{1,0:T(8,128)(2,1)S(1)} %copy-done.1), custom_call_target="tpu_custom_call" | custom-call | tf_op jit(solution)/shard_map/correlate/pallas_call | solution.py:552
Async XLA Ops:
  0.8 10.0 %collective-permute-start = (bf16[4,64,128]{2,1,0:T(8,128)(2,1)S(1)}, bf16[4,64,128]{2,1,0:T(8,128)(2,1)S(1)}, u32[]{:S(2)}, u32[]{:S(2)}) collective-permute-start(bf16[4,64,128]{2,1,0:T(8,128)(2,1)S(1)} %slice.3), channel_id=1, source_target_pairs={{0,1},{1,2},{2,3},{3,4},{4,5},{5,6},{6,7},{7,8},{8,9},{9,10},{10,1... | collective-permute-start | bytes 196616 | tf_op jit(solution)/shard_map/ppermute | solution.py:581
  10.8 1.2 %copy-start = (bf16[4,64,2048]{2,1,0:T(8,128)(2,1)S(1)}, bf16[4,64,2048]{2,1,0:T(8,128)(2,1)}, u32[]{:S(2)}) copy-start(bf16[4,64,2048]{2,1,0:T(8,128)(2,1)} %col_ref.1) | copy-start | bytes 3145732
  12.0 1.0 %copy-start.3 = (bf16[640,256]{1,0:T(8,128)(2,1)S(1)}, bf16[640,256]{1,0:T(8,128)(2,1)}, u32[]{:S(2)}) copy-start(bf16[640,256]{1,0:T(8,128)(2,1)} %constant.20.clone.taps_ref) | copy-start | bytes 983044
  13.0 0.9 copy-start.6
  13.9 0.9 copy-start.7
  14.8 0.7 copy-start.8
  15.5 0.7 copy-start.9
  16.3 0.7 copy-start.10
  16.9 52.5 %copy-start.1 = (bf16[1024,896]{1,0:T(8,128)(2,1)S(1)}, bf16[1024,896]{1,0:T(8,128)(2,1)}, u32[]{:S(2)}) copy-start(bf16[1024,896]{1,0:T(8,128)(2,1)} %constant.25.clone.lag_ref) | copy-start | bytes 5505028
  20.2 0.7 copy-start.4
  20.8 0.7 copy-start.5
  69.5 1.2 %copy-start.2 = (bf16[32,128,128]{2,1,0:T(8,128)(2,1)S(1)}, bf16[32,128,128]{2,1,0:T(8,128)(2,1)}, u32[]{:S(2)}) copy-start(bf16[32,128,128]{2,1,0:T(8,128)(2,1)} %get-tuple-element.12.col_ref) | copy-start | bytes 3145732

commit v3 on v2

--- a/solution.py
+++ b/solution.py
@@ -43,35 +43,36 @@
 )
 
 
-def split_np(table):
-    high = table.astype(ml_dtypes.bfloat16)
-    low = (table - high.astype(np.float64)).astype(ml_dtypes.bfloat16)
-    return high, low
-
-
-def filter_table():
-    index = np.arange(TAPS, dtype=np.float64)
-    centred = (index - (TAPS - 1) / 2.0) / DECIM
-    window = 0.5 * (1.0 - np.cos(2.0 * np.pi * (index + 0.5) / TAPS))
-    taps = window * np.sin(np.pi * centred) / (np.pi * centred) / DECIM
-    table = np.zeros((5 * LANE, LANE))
-    for j in range(LANE):
-        table[TAPS + DECIM * j : 2 * TAPS + DECIM * j, j] = taps
-    high, low = split_np(table)
-    return np.concatenate([high, low], axis=1)
-
-
-def turn_tables():
-    sample = np.arange(SEG)
-    coarse = (8 * np.arange(BINS // 8))[:, None] * sample[None, :] % NFT
-    fine = np.arange(8)[:, None] * sample[None, :] % NFT
-    pick = lambda fn, phase: fn(phase * TWO_PI).astype(np.float32)
-    return (
-        pick(np.cos, coarse),
-        pick(np.sin, coarse),
-        pick(np.cos, fine),
-        pick(np.sin, fine),
-    )
+def turns(rows, step, columns):
+    row = lax.broadcasted_iota(jnp.int32, (rows, columns), 0) * step
+    index = (row * lax.broadcasted_iota(jnp.int32, (rows, columns), 1)) & (NFT - 1)
+    index = jnp.where(index >= NFT // 2, index - NFT, index)
+    phase = index.astype(F32) * TWO_PI
+    return jnp.cos(phase), jnp.sin(phase)
+
+
+def fill_taps(taps_ref):
+    row = lax.broadcasted_iota(jnp.int32, (8, LANE), 0)
+    lane = lax.broadcasted_iota(jnp.int32, (8, LANE), 1)
+    index = row - TAPS - DECIM * (lane - LANE)
+    inside = (index >= 0) & (index < TAPS)
+    position = jnp.where(inside, index, 0).astype(F32)
+    centred = (position - (TAPS - 1) / 2.0) * (1.0 / DECIM)
+    window = 0.5 * (1.0 - jnp.cos((2.0 * math.pi / TAPS) * (position + 0.5)))
+    turn = math.pi * centred
+    value = jnp.where(inside, window * jnp.sin(turn) / turn * (1.0 / DECIM), 0.0)
+    shift = 8 // DECIM
+    for r in range(0, 5 * LANE // 8, 2):
+        pair = []
+        for one in (r, r + 1):
+            moved = value
+            if one * shift % LANE:
+                moved = pltpu.roll(value, one * shift % LANE, 1)
+            offset = row - TAPS - DECIM * (lane - one * shift)
+            pair.append(jnp.where((offset >= 0) & (offset < TAPS), moved, 0.0))
+        high, low = split(jnp.concatenate(pair, axis=0))
+        taps_ref[8 * r : 8 * r + 16, :LANE] = high
+        taps_ref[8 * r : 8 * r + 16, LANE:] = low
 
 
 def bin_order():
@@ -100,24 +101,27 @@
 
 
 def prepare_kernel(
-    blocks, live, row_ref, col_ref, row_tail, col_tail, taps_ref,
-    coarse_cos, coarse_sin, fine_cos, fine_sin,
-    row_out, col_out, fwd_high, fwd_low, padded,
+    blocks, live, row_ref, col_ref, row_tail, col_tail,
+    row_out, col_out, taps_ref, fwd_high, fwd_low, padded,
 ):
     del blocks
-    fc, fs = fine_cos[...], fine_sin[...]
-    for a in range(BINS // 8):
-        cc = coarse_cos[a : a + 1, :]
-        cs = coarse_sin[a : a + 1, :]
-        rows = slice(8 * a, 8 * a + 8)
-        for value, base in ((cc * fc - cs * fs, 0), (-(cs * fc + cc * fs), BINS)):
-            high, low = split(value)
-            fwd_high[base + rows.start : base + rows.stop, :] = high
-            fwd_low[base + rows.start : base + rows.stop, :] = low
+    fill_taps(taps_ref)
+    coarse_cos, coarse_sin = turns(BINS // 8, 8, SEG)
+    fine_cos, fine_sin = turns(8, 1, SEG)
+    for a in range(0, BINS // 8, 2):
+        reals, imags = [], []
+        for one in (a, a + 1):
+            cc, cs = coarse_cos[one : one + 1, :], coarse_sin[one : one + 1, :]
+            reals.append(cc * fine_cos - cs * fine_sin)
+            imags.append(-(cs * fine_cos + cc * fine_sin))
+        for value, base in ((reals, 8 * a), (imags, BINS + 8 * a)):
+            high, low = split(jnp.concatenate(value, axis=0))
+            fwd_high[base : base + 16, :] = high
+            fwd_low[base : base + 16, :] = low
 
     record = jnp.concatenate([row_ref[0], col_ref[0]], axis=0)
     tail = jnp.concatenate([row_tail[0], col_tail[0]], axis=0)
-    count = live[0]
+    count = live[lax.axis_index("tm")]
     lane = lax.broadcasted_iota(jnp.int32, (1, LANE), 1)
     pieces = []
     for b in range(SEG // LANE):
@@ -173,8 +177,6 @@
 def prepare(records, tails, tile_blocks, live):
     stations, length = records.shape[1], records.shape[2]
     whole = lambda *shape: pl.BlockSpec(shape, lambda i, b, l: (0,) * len(shape))
-    taps = jnp.asarray(filter_table())
-    tables = [jnp.asarray(table) for table in turn_tables()]
     return pl.pallas_call(
         prepare_kernel,
         grid_spec=pltpu.PrefetchScalarGridSpec(
@@ -185,14 +187,10 @@
                 pl.BlockSpec((1, stations, length), lambda i, b, l: (b[1], 0, 0)),
                 pl.BlockSpec((1, stations, LANE), lambda i, b, l: (b[0], 0, 0)),
                 pl.BlockSpec((1, stations, LANE), lambda i, b, l: (b[1], 0, 0)),
-                whole(5 * LANE, 2 * LANE),
-                whole(BINS // 8, SEG),
-                whole(BINS // 8, SEG),
-                whole(8, SEG),
-                whole(8, SEG),
             ],
             out_specs=[whole(BINS, LANE), whole(4, LANE, LANE)],
             scratch_shapes=[
+                pltpu.VMEM((5 * LANE, 2 * LANE), BF16),
                 pltpu.VMEM((2 * BINS, SEG), BF16),
                 pltpu.VMEM((2 * BINS, SEG), BF16),
                 pltpu.VMEM((BINS + 16, LANE), F32),
@@ -204,7 +202,7 @@
         ],
         compiler_params=pltpu.CompilerParams(vmem_limit_bytes=40 << 20),
         name="prepare",
-    )(tile_blocks, live, records, records, tails, tails, taps, *tables)
+    )(tile_blocks, live, records, records, tails, tails)
 
 
 class Place:
@@ -457,7 +455,7 @@
     dma = pltpu.SemaphoreType.DMA
     return pl.pallas_call(
         exchange_kernel,
-        in_specs=[anywhere, anywhere],
+        in_specs=[pl.BlockSpec(memory_space=pltpu.VMEM)] * 2,
         out_specs=[anywhere, anywhere],
         out_shape=[
             jax.ShapeDtypeStruct((32,) + row_own.shape, BF16),
@@ -473,16 +471,18 @@
     )(row_own, col_own)
 
 
-def correlate_kernel(segments, row_ref, col_ref, lag_ref, out_ref, rows, cols, cross, stacked):
+def correlate_kernel(segments, row_ref, col_ref, lag_ref, out_ref, rows, cols, cross, stacked, spare):
     step = pl.program_id(0)
     half = LANE // 2
     group = 8
     count_k = QUARTERS * KCHUNK
+    stride_k, stride_c, stride_p = count_k + 8, KCHUNK + 8, half + 8
 
     @pl.when(step < CHUNKS)
     def _():
-        rows[...] = row_ref[...].reshape(segments * count_k, LANE).astype(F32)
-        cols[...] = col_ref[...].reshape(segments * KCHUNK, LANE).astype(F32)
+        for g in range(segments):
+            rows[g * stride_k : g * stride_k + count_k, :] = row_ref[g].reshape(count_k, LANE).astype(F32)
+            cols[g * stride_c : g * stride_c + KCHUNK, :] = col_ref[g].astype(F32)
         lane = lax.broadcasted_iota(jnp.int32, (32, group * segments), 1)
         sign = jnp.where(
             lax.broadcasted_iota(jnp.int32, (1, LANE), 1) < half, 1.0, -1.0
@@ -490,7 +490,7 @@
         for block in range(KCHUNK // group):
             gathered = jnp.concatenate(
                 [
-                    cols[pl.ds(block * group + b, segments, stride=KCHUNK), :]
+                    cols[pl.ds(block * group + b, segments, stride=stride_c), :]
                     for b in range(group)
                 ],
                 axis=0,
@@ -511,7 +511,7 @@
                 base = quarter * KCHUNK + block * group
                 right = jnp.concatenate(
                     [
-                        rows[pl.ds(base + b, segments, stride=count_k), :]
+                        rows[pl.ds(base + b, segments, stride=stride_k), :]
                         for b in range(group)
                     ],
                     axis=0,
@@ -521,29 +521,34 @@
                     top = product[b * 32 : b * 32 + 16, :]
                     low = product[b * 32 + 16 : b * 32 + 32, :]
                     value = top + sign * pltpu.roll(low, half, 1)
-                    cross[pl.ds(base + b, 16, stride=count_k), :] = value
+                    cross[pl.ds(base + b, 16, stride=stride_k), :] = value
+        at = pl.multiple_of(step * count_k, LANE)
         for q in range(16):
-            turned = cross[q * count_k : (q + 1) * count_k, :].T.astype(BF16)
-            for chunk in range(CHUNKS):
-
-                @pl.when(step == chunk)
-                def _():
-                    at = chunk * count_k
-                    stacked[q * half : (q + 1) * half, at : at + count_k] = turned[:half]
-                    stacked[q * half : (q + 1) * half, BINS + at : BINS + at + count_k] = turned[half:]
+            turned = cross[q * stride_k : q * stride_k + count_k, :].astype(BF16).T
+            stacked[q * half : (q + 1) * half, pl.ds(at, count_k)] = turned[:half]
+            stacked[q * half : (q + 1) * half, pl.ds(BINS + at, count_k)] = turned[half:]
 
     @pl.when(step >= CHUNKS)
     def _():
-        for q in range(16):
-            value = dot(stacked[q * half : (q + 1) * half, :], lag_ref[...])
-            out_ref[pl.ds(q, half, stride=16), :] = value
+        for r in range(1):
+            value = dot(stacked[...], lag_ref[...])
+            for q in range(16):
+                for side in range(2):
+                    spare[side, (q) * 72 : (q) * 72 + half, :] = value[
+                        q * half : (q + 1) * half, side * LANE : (side + 1) * LANE
+                    ]
+        for p in range(half):
+            for side in range(2):
+                out_ref[p * 16 : p * 16 + 16, side * LANE : (side + 1) * LANE] = spare[
+                    side, pl.ds(p, 16, stride=stride_p), :
+                ]
 
 
 def correlate(row_all, col_all):
     segments = row_all.shape[0]
     row_all = row_all.reshape(segments, QUARTERS, LANE, LANE)
     table = lag_table()
-    width = LANE
+    width = 2 * LANE
     tiles = -(-LAGS // width)
     table = jnp.asarray(np.pad(table, ((0, 0), (0, tiles * width - LAGS))))
     pairs = 16 * (LANE // 2)
@@ -565,10 +570,11 @@
         out_specs=pl.BlockSpec((pairs, width), lambda i: (0, jnp.maximum(i - CHUNKS, 0))),
         out_shape=jax.ShapeDtypeStruct((pairs, LAGS), F32),
         scratch_shapes=[
-            pltpu.VMEM((segments * QUARTERS * KCHUNK, LANE), F32),
-            pltpu.VMEM((segments * KCHUNK, LANE), F32),
-            pltpu.VMEM((16 * QUARTERS * KCHUNK, LANE), F32),
+            pltpu.VMEM((segments * (QUARTERS * KCHUNK + 8), LANE), F32),
+            pltpu.VMEM((segments * (KCHUNK + 8), LANE), F32),
+            pltpu.VMEM((16 * (QUARTERS * KCHUNK + 8), LANE), F32),
             pltpu.VMEM((pairs, 2 * BINS), BF16),
+            pltpu.VMEM((2, 16 * 72, LANE), F32),
         ],
         compiler_params=pltpu.CompilerParams(vmem_limit_bytes=48 << 20),
         name="correlate",
@@ -581,8 +587,7 @@
     tails = lax.ppermute(
         records[:, :, length - LANE :], "tm", [(i, i + 1) for i in range(size - 1)]
     )
-    live = lax.dynamic_slice(live_len, (lax.axis_index("tm"),), (1,))
-    row_own, col_own = prepare(records, tails, tile_blocks, live)
+    row_own, col_own = prepare(records, tails, tile_blocks, live_len)
     row_all, col_all = exchange(row_own, col_own)
     result = correlate(row_all, col_all)
     return result.reshape(LANE // 2, 16, LAGS)

time: 96.5 us -> 79.1 us (0.82)
  Pallas kernels: 76.5 us -> 62.9 us
  local copies, waits for them, and re-layouts: 10.7 us -> 5.9 us
  waiting for transfers between devices: 6.81 us -> 8.06 us
    pallas_call x1, Pallas kernels: 25.3 us -> 11 us  [correlate(): pl.pallas_call(body, grid=(CHUNKS + tiles,), in_specs=[pl.BlockSpec((segm...]
    unnamed x22 -> x14, local copies, waits for them, and re-layouts: 8.62 us -> 5.06 us
    ppermute x1, waiting for transfers between devices: 6.81 us -> 8.06 us  [shards(): lax.ppermute(records[:, :, length - LANE:], 'tm', [(i, i + 1) for i in ra...]
    dynamic_slice x1 -> x0, local copies, waits for them, and re-layouts: 1.24 us -> none  [shards(): live = lax.dynamic_slice(live_len, (lax.axis_index('tm'),), (1,))]
  transfers between devices with their start and end apart: 1 -> 1, of which waited for: 1 -> 1; matrix products, arithmetic and copies ran while one was open for 1% -> 0% of each run, Pallas kernels for 0% -> 0%
where the time goes in v3:
time: 79.1 us; the launch traced here: 78.9 us
  Pallas kernels  62.9 us (80%)
  waiting for transfers between devices  8.06 us (10%)
  local copies, waits for them, and re-layouts  5.9 us (7%)
  starting transfers between devices  1.91 us (2%)
    pallas_call x1, Pallas kernels, exchange(): pl.pallas_call(exchange_kernel, in_specs=[pl.BlockSpec(memory_space=pltpu...  48.7 us
    pallas_call x1, Pallas kernels, correlate(): pl.pallas_call(body, grid=(CHUNKS + tiles,), in_specs=[pl.BlockSpec((segm...  11 us
    ppermute x1, waiting for transfers between devices, shards(): lax.ppermute(records[:, :, length - LANE:], 'tm', [(i, i + 1) for i in ra...  8.06 us
    unnamed x14, local copies, waits for them, and re-layouts  5.06 us
    pallas_call x1, Pallas kernels, prepare(): pl.pallas_call(prepare_kernel, grid_spec=pltpu.PrefetchScalarGridSpec(num...  3.21 us
    ppermute x1, starting transfers between devices, shards(): lax.ppermute(records[:, :, length - LANE:], 'tm', [(i, i + 1) for i in ra...  1.91 us
  transfers between devices with their start and end apart: 1, of which 1 were waited for; matrix products, arithmetic and copies ran while one was open for 0% of the time, Pallas kernels for 0%

profile of v3, /device:TPU:14, one launch (start us, length us, event | category | flops | bytes accessed | tf_op | source)
XLA Modules:
  0.0 78.9 jit_solution(4637930896350694308)
XLA Ops:
  0.0 0.8 %slice.3 = bf16[4,64,128]{2,1,0:T(8,128)(2,1)S(1)} slice(bf16[4,64,2048]{2,1,0:T(8,128)(2,1)} %col_ref.1), slice={[0:4], [0:64], [1920:2048]} | slice | bytes 131072 | tf_op jit(solution)/shard_map/slice | solution.py:588
  0.8 1.9 %collective-permute-start = (bf16[4,64,128]{2,1,0:T(8,128)(2,1)S(1)}, bf16[4,64,128]{2,1,0:T(8,128)(2,1)S(1)}, u32[]{:S(2)}, u32[]{:S(2)}) collective-permute-start(bf16[4,64,128]{2,1,0:T(8,128)(2,1)S(1)} %slice.3), channel_id=1, source_target_pairs={{0,1},{1,2},{2,3},{3,4},{4,5},{5,6},{6,7},{7,8},{8,9},{9,10},{10,1... | collective-permute-start | bytes 196616 | tf_op jit(solution)/shard_map/ppermute | solution.py:587
  2.8 8.1 %collective-permute-done.row_tail.col_tail = bf16[4,64,128]{2,1,0:T(8,128)(2,1)S(1)} collective-permute-done((bf16[4,64,128]{2,1,0:T(8,128)(2,1)S(1)}, bf16[4,64,128]{2,1,0:T(8,128)(2,1)S(1)}, u32[]{:S(2)}, u32[]{:S(2)}) %collective-permute-start) | collective-permute-done | bytes 65568 | tf_op jit(solution)/shard_map/ppermute | solution.py:587
  10.8 0.0 copy-start
  10.8 1.2 %copy-done = bf16[4,64,2048]{2,1,0:T(8,128)(2,1)S(1)} copy-done((bf16[4,64,2048]{2,1,0:T(8,128)(2,1)S(1)}, bf16[4,64,2048]{2,1,0:T(8,128)(2,1)}, u32[]{:S(2)}) %copy-start) | copy-done | bytes 1048600
  12.0 0.0 copy-start.5
  12.1 0.7 copy-done.5
  12.7 0.0 copy-start.6
  12.7 0.7 copy-done.6
  13.4 0.0 copy-start.1
  13.4 3.2 %prepare.1 = (bf16[512,128]{1,0:T(8,128)(2,1)S(1)}, bf16[4,128,128]{2,1,0:T(8,128)(2,1)S(1)}) custom-call(s32[2]{0:T(128)S(1)} %copy-done.5, s32[32]{0:T(128)S(1)} %copy-done.6, bf16[4,64,2048]{2,1,0:T(8,128)(2,1)S(1)} %copy-done, bf16[4,64,2048]{2,1,0:T(8,128)(2,1)S(1)} %copy-done, bf16[4,64,128]{2,1,0:T(8,128)(2,1)S(1)} %collective-permute-done.row_tail.col_tail, ...), custom_call_target="tpu_custom_call" | custom-call | tf_op jit(solution)/shard_map/prepare/pallas_call | solution.py:180
  16.6 0.0 copy-start.3
  16.6 0.6 copy-done.3
  17.2 0.0 copy-start.4
  17.2 0.6 copy-done.4
  17.9 48.7 %exchange.1 = (bf16[32,512,128]{2,1,0:T(8,128)(2,1)}, bf16[32,128,128]{2,1,0:T(8,128)(2,1)}) custom-call(bf16[512,128]{1,0:T(8,128)(2,1)} %copy-done.3, bf16[4,128,128]{2,1,0:T(8,128)(2,1)} %copy-done.4), custom_call_target="tpu_custom_call" | custom-call | tf_op jit(solution)/shard_map/exchange/pallas_call | solution.py:456
  66.6 0.0 copy-done.1
  66.6 0.0 copy-start.2
  66.6 1.2 %copy-done.2 = bf16[32,128,128]{2,1,0:T(8,128)(2,1)S(1)} copy-done((bf16[32,128,128]{2,1,0:T(8,128)(2,1)S(1)}, bf16[32,128,128]{2,1,0:T(8,128)(2,1)}, u32[]{:S(2)}) %copy-start.2) | copy-done | bytes 1048600
  67.9 11.0 %correlate.1 = f32[1024,801]{1,0:T(8,128)} custom-call(bf16[32,4,128,128]{3,2,1,0:T(8,128)(2,1)} %bitcast.2, bf16[32,128,128]{2,1,0:T(8,128)(2,1)S(1)} %copy-done.2, bf16[1024,1024]{1,0:T(8,128)(2,1)S(1)} %copy-done.1), custom_call_target="tpu_custom_call" | custom-call | tf_op jit(solution)/shard_map/correlate/pallas_call | solution.py:557
Async XLA Ops:
  0.8 10.0 %collective-permute-start = (bf16[4,64,128]{2,1,0:T(8,128)(2,1)S(1)}, bf16[4,64,128]{2,1,0:T(8,128)(2,1)S(1)}, u32[]{:S(2)}, u32[]{:S(2)}) collective-permute-start(bf16[4,64,128]{2,1,0:T(8,128)(2,1)S(1)} %slice.3), channel_id=1, source_target_pairs={{0,1},{1,2},{2,3},{3,4},{4,5},{5,6},{6,7},{7,8},{8,9},{9,10},{10,1... | collective-permute-start | bytes 196616 | tf_op jit(solution)/shard_map/ppermute | solution.py:587
  10.8 1.2 %copy-start = (bf16[4,64,2048]{2,1,0:T(8,128)(2,1)S(1)}, bf16[4,64,2048]{2,1,0:T(8,128)(2,1)}, u32[]{:S(2)}) copy-start(bf16[4,64,2048]{2,1,0:T(8,128)(2,1)} %col_ref.1) | copy-start | bytes 3145732
  12.0 0.7 copy-start.5
  12.7 0.7 copy-start.6
  13.4 53.3 %copy-start.1 = (bf16[1024,1024]{1,0:T(8,128)(2,1)S(1)}, bf16[1024,1024]{1,0:T(8,128)(2,1)}, u32[]{:S(2)}) copy-start(bf16[1024,1024]{1,0:T(8,128)(2,1)} %constant.2.clone.lag_ref) | copy-start | bytes 6291460
  16.6 0.7 copy-start.3
  17.2 0.7 copy-start.4
  66.6 1.2 %copy-start.2 = (bf16[32,128,128]{2,1,0:T(8,128)(2,1)S(1)}, bf16[32,128,128]{2,1,0:T(8,128)(2,1)}, u32[]{:S(2)}) copy-start(bf16[32,128,128]{2,1,0:T(8,128)(2,1)} %get-tuple-element.12.col_ref) | copy-start | bytes 3145732

commit v4 on v3

--- a/solution.py
+++ b/solution.py
@@ -1,4 +1,3 @@
-import functools
 import math
 
 import jax
@@ -22,6 +21,10 @@
 QUARTERS = 4
 CHUNKS = 4
 KCHUNK = LANE // CHUNKS
+PAIRS = 1024
+STRIDE_K = QUARTERS * KCHUNK + 8
+STRIDE_C = KCHUNK + 8
+STRIDE_P = LANE // 2 + 8
 TWO_PI = 2.0 * math.pi / NFT
 F32 = jnp.float32
 BF16 = jnp.bfloat16
@@ -100,12 +103,7 @@
     return lax.dot_general(a, b, (dims, ((), ())), preferred_element_type=F32)
 
 
-def prepare_kernel(
-    blocks, live, row_ref, col_ref, row_tail, col_tail,
-    row_out, col_out, taps_ref, fwd_high, fwd_low, padded,
-):
-    del blocks
-    fill_taps(taps_ref)
+def fill_transform(fwd_high, fwd_low):
     coarse_cos, coarse_sin = turns(BINS // 8, 8, SEG)
     fine_cos, fine_sin = turns(8, 1, SEG)
     for a in range(0, BINS // 8, 2):
@@ -119,20 +117,8 @@
             fwd_high[base : base + 16, :] = high
             fwd_low[base : base + 16, :] = low
 
-    record = jnp.concatenate([row_ref[0], col_ref[0]], axis=0)
-    tail = jnp.concatenate([row_tail[0], col_tail[0]], axis=0)
-    count = live[lax.axis_index("tm")]
-    lane = lax.broadcasted_iota(jnp.int32, (1, LANE), 1)
-    pieces = []
-    for b in range(SEG // LANE):
-        span = DECIM * LANE
-        before = tail if b == 0 else record[:, b * span - LANE : b * span]
-        both = dot(before, taps_ref[:LANE, :]) + dot(
-            record[:, b * span : (b + 1) * span], taps_ref[LANE:, :]
-        )
-        value = both[:, :LANE] + both[:, LANE:]
-        pieces.append(jnp.where(lane + b * LANE < count, value, 0.0))
-    filtered = jnp.concatenate(pieces, axis=1)
+
+def whiten(filtered, fwd_high, fwd_low, padded):
     high, low = split(filtered)
     last = ((1,), (1,))
     spectra = (
@@ -152,11 +138,18 @@
     mean = jnp.sum(amplitude, axis=0, keepdims=True) * (1.0 / BINS)
     level = smooth * (1.0 / (2 * SMOOTH + 1)) + 0.05 * mean + 1e-06
     inverse = 1.0 / level
-    real = real * inverse
-    imag = imag * inverse
+    return real * inverse, imag * inverse
+
+
+def pack_rows(real, imag, row_own):
     half = LANE // 2
     lower = lax.broadcasted_iota(jnp.int32, (BINS, LANE), 1) < half
-    row_out[...] = jnp.where(lower, real, pltpu.roll(imag, half, 1)).astype(BF16)
+    row_own[...] = jnp.where(lower, real, pltpu.roll(imag, half, 1)).astype(BF16)
+
+
+def pack_columns(real, imag, col_own):
+    half = LANE // 2
+    lower = lax.broadcasted_iota(jnp.int32, (BINS, LANE), 1) < half
     cols = jnp.where(lower, pltpu.roll(real, half, 1), imag)
     lanes = lax.broadcasted_iota(jnp.int32, (LANE, LANE), 1)
     for j in range(4):
@@ -171,38 +164,7 @@
                     moved = pltpu.roll(part, (target - source) % LANE, 1)
                 keep = (lanes >= target) & (lanes < target + 16)
                 total = jnp.where(keep, moved, total)
-        col_out[j] = total.astype(BF16)
-
-
-def prepare(records, tails, tile_blocks, live):
-    stations, length = records.shape[1], records.shape[2]
-    whole = lambda *shape: pl.BlockSpec(shape, lambda i, b, l: (0,) * len(shape))
-    return pl.pallas_call(
-        prepare_kernel,
-        grid_spec=pltpu.PrefetchScalarGridSpec(
-            num_scalar_prefetch=2,
-            grid=(1,),
-            in_specs=[
-                pl.BlockSpec((1, stations, length), lambda i, b, l: (b[0], 0, 0)),
-                pl.BlockSpec((1, stations, length), lambda i, b, l: (b[1], 0, 0)),
-                pl.BlockSpec((1, stations, LANE), lambda i, b, l: (b[0], 0, 0)),
-                pl.BlockSpec((1, stations, LANE), lambda i, b, l: (b[1], 0, 0)),
-            ],
-            out_specs=[whole(BINS, LANE), whole(4, LANE, LANE)],
-            scratch_shapes=[
-                pltpu.VMEM((5 * LANE, 2 * LANE), BF16),
-                pltpu.VMEM((2 * BINS, SEG), BF16),
-                pltpu.VMEM((2 * BINS, SEG), BF16),
-                pltpu.VMEM((BINS + 16, LANE), F32),
-            ],
-        ),
-        out_shape=[
-            jax.ShapeDtypeStruct((BINS, LANE), BF16),
-            jax.ShapeDtypeStruct((4, LANE, LANE), BF16),
-        ],
-        compiler_params=pltpu.CompilerParams(vmem_limit_bytes=40 << 20),
-        name="prepare",
-    )(tile_blocks, live, records, records, tails, tails)
+        col_own[j] = total.astype(BF16)
 
 
 class Place:
@@ -237,9 +199,11 @@
     return [(kind, arg) for _, kind, arg in events]
 
 
-def exchange_kernel(
-    row_ref, col_ref, row_all, col_all, stage,
-    row_send, row_recv, near_send, near_recv, stage_send, stage_recv,
+def spectra_kernel(
+    blocks, live, records, stacked,
+    tail_own, tail_in, taps_ref, fwd_high, fwd_low, padded, row_ref, col_ref,
+    row_all, col_all, stage, rows, cols, cross,
+    tail_sem, row_send, row_recv, near_send, near_recv, stage_send, stage_recv,
     col_send, col_recv, local_sem,
 ):
     me = Place()
@@ -269,13 +233,57 @@
     greet(me.at(xh=1 - me.xh, xl=1 - me.xl))
     greet(me.at(y=up))
     greet(me.at(y=down))
-    pl.semaphore_wait(barrier, 2 * RING - 1 + 5)
+    greet(me.at(xh=1 - me.xh, z=RING - 1 - me.z, c=1 - me.c))
 
     def remote(src, dst, send, recv, device):
         return pltpu.make_async_remote_copy(
             src_ref=src, dst_ref=dst, send_sem=send, recv_sem=recv,
             device_id=device, device_id_type=MESH,
         )
+
+    fill_taps(taps_ref)
+    fill_transform(fwd_high, fwd_low)
+    length = records.shape[2]
+    stations = records.shape[1]
+    for side in range(2):
+        tail_own[side * stations : (side + 1) * stations, :] = records[
+            blocks[side], :, length - LANE :
+        ]
+    pl.semaphore_wait(barrier, 2 * RING - 1 + 6)
+
+    tm = lax.axis_index("tm")
+    after = lax.rem(tm + 1, 4 * RING)
+    tail_copy = remote(
+        tail_own, tail_in, tail_sem.at[0], tail_sem.at[1],
+        {"pair": lax.axis_index("pair"), "tm": after},
+    )
+    pl.when(tm < 4 * RING - 1)(tail_copy.start)
+    count = live[tm]
+    lane = lax.broadcasted_iota(jnp.int32, (1, LANE), 1)
+    record = jnp.concatenate([records[blocks[0]], records[blocks[1]]], axis=0)
+    span = DECIM * LANE
+    pieces = []
+    for b in range(SEG // LANE):
+        both = dot(record[:, b * span : (b + 1) * span], taps_ref[LANE:, :])
+        if b > 0:
+            both = both + dot(record[:, b * span - LANE : b * span], taps_ref[:LANE, :])
+        pieces.append(both)
+
+    @pl.when(tm == 0)
+    def _():
+        tail_in[...] = jnp.zeros_like(tail_in)
+
+    pl.when(tm > 0)(tail_copy.wait_recv)
+    pieces[0] = pieces[0] + dot(tail_in[...], taps_ref[:LANE, :])
+    filtered = jnp.concatenate(
+        [
+            jnp.where(lane + b * LANE < count, both[:, :LANE] + both[:, LANE:], 0.0)
+            for b, both in enumerate(pieces)
+        ],
+        axis=1,
+    )
+    real, imag = whiten(filtered, fwd_high, fwd_low, padded)
+    pack_columns(real, imag, col_ref)
 
     pending = []
 
@@ -300,6 +308,7 @@
         def _():
             pltpu.make_async_copy(col_ref.at[j], stage.at[index], stage_recv.at[index]).start()
 
+    pack_rows(real, imag, row_ref)
     own = slot_of(me.xh, me.c, me.z)
     own_local = pltpu.make_async_copy(row_ref, row_all.at[own], local_sem.at[2 * RING])
 
@@ -448,148 +457,138 @@
             copy.wait_send()
         else:
             pl.when(when)(copy.wait_send)
-
-
-def exchange(row_own, col_own):
-    anywhere = pl.BlockSpec(memory_space=pl.ANY)
-    dma = pltpu.SemaphoreType.DMA
-    return pl.pallas_call(
-        exchange_kernel,
-        in_specs=[pl.BlockSpec(memory_space=pltpu.VMEM)] * 2,
-        out_specs=[anywhere, anywhere],
-        out_shape=[
-            jax.ShapeDtypeStruct((32,) + row_own.shape, BF16),
-            jax.ShapeDtypeStruct((32,) + col_own.shape[1:], BF16),
-        ],
-        scratch_shapes=[
-            pltpu.VMEM((2 * RING,) + col_own.shape[1:], BF16),
-            dma((3, 8, PARTS)), dma((32, PARTS)), dma((2, 8, PARTS)), dma((32, PARTS)),
-            dma((4,)), dma((2 * RING,)), dma((32, 2)), dma((32,)), dma((2 * RING + 1,)),
-        ],
-        compiler_params=pltpu.CompilerParams(collective_id=0, has_side_effects=True),
-        name="exchange",
-    )(row_own, col_own)
-
-
-def correlate_kernel(segments, row_ref, col_ref, lag_ref, out_ref, rows, cols, cross, stacked, spare):
-    step = pl.program_id(0)
+    pl.when(tm < 4 * RING - 1)(tail_copy.wait_send)
+
+    @pl.loop(0, CHUNKS)
+    def _(chunk):
+        cross_chunk(chunk, row_all, col_all, rows, cols, cross, stacked)
+
+
+def cross_chunk(chunk, row_all, col_all, rows, cols, cross, stacked):
+    segments = row_all.shape[0]
     half = LANE // 2
     group = 8
     count_k = QUARTERS * KCHUNK
-    stride_k, stride_c, stride_p = count_k + 8, KCHUNK + 8, half + 8
-
-    @pl.when(step < CHUNKS)
-    def _():
-        for g in range(segments):
-            rows[g * stride_k : g * stride_k + count_k, :] = row_ref[g].reshape(count_k, LANE).astype(F32)
-            cols[g * stride_c : g * stride_c + KCHUNK, :] = col_ref[g].astype(F32)
-        lane = lax.broadcasted_iota(jnp.int32, (32, group * segments), 1)
-        sign = jnp.where(
-            lax.broadcasted_iota(jnp.int32, (1, LANE), 1) < half, 1.0, -1.0
-        ).astype(F32)
-        for block in range(KCHUNK // group):
-            gathered = jnp.concatenate(
+    first = pl.multiple_of(chunk * KCHUNK, KCHUNK)
+    for g in range(segments):
+        for quarter in range(QUARTERS):
+            at = g * STRIDE_K + quarter * KCHUNK
+            rows[at : at + KCHUNK, :] = row_all[
+                g, pl.ds(quarter * LANE + first, KCHUNK), :
+            ].astype(F32)
+        cols[g * STRIDE_C : g * STRIDE_C + KCHUNK, :] = col_all[
+            g, pl.ds(first, KCHUNK), :
+        ].astype(F32)
+    lane = lax.broadcasted_iota(jnp.int32, (32, group * segments), 1)
+    sign = jnp.where(
+        lax.broadcasted_iota(jnp.int32, (1, LANE), 1) < half, 1.0, -1.0
+    ).astype(F32)
+    for block in range(KCHUNK // group):
+        gathered = jnp.concatenate(
+            [cols[pl.ds(block * group + b, segments, stride=STRIDE_C), :] for b in range(group)],
+            axis=0,
+        )
+        turned = gathered.T.astype(BF16)
+        for quarter in range(QUARTERS):
+            left = turned[quarter * 32 : quarter * 32 + 32, :]
+            zero = jnp.zeros_like(left)
+            wide = jnp.concatenate(
                 [
-                    cols[pl.ds(block * group + b, segments, stride=stride_c), :]
+                    jnp.where((lane >= b * segments) & (lane < (b + 1) * segments), left, zero)
                     for b in range(group)
                 ],
                 axis=0,
             )
-            turned = gathered.T.astype(BF16)
-            for quarter in range(QUARTERS):
-                left = turned[quarter * 32 : quarter * 32 + 32, :]
-                zero = jnp.zeros_like(left)
-                wide = jnp.concatenate(
-                    [
-                        jnp.where(
-                            (lane >= b * segments) & (lane < (b + 1) * segments), left, zero
-                        )
-                        for b in range(group)
-                    ],
-                    axis=0,
+            base = quarter * KCHUNK + block * group
+            right = jnp.concatenate(
+                [rows[pl.ds(base + b, segments, stride=STRIDE_K), :] for b in range(group)],
+                axis=0,
+            ).astype(BF16)
+            product = dot(wide, right)
+            for b in range(group):
+                top = product[b * 32 : b * 32 + 16, :]
+                low = product[b * 32 + 16 : b * 32 + 32, :]
+                cross[pl.ds(base + b, 16, stride=STRIDE_K), :] = top + sign * pltpu.roll(
+                    low, half, 1
                 )
-                base = quarter * KCHUNK + block * group
-                right = jnp.concatenate(
-                    [
-                        rows[pl.ds(base + b, segments, stride=stride_k), :]
-                        for b in range(group)
-                    ],
-                    axis=0,
-                ).astype(BF16)
-                product = dot(wide, right)
-                for b in range(group):
-                    top = product[b * 32 : b * 32 + 16, :]
-                    low = product[b * 32 + 16 : b * 32 + 32, :]
-                    value = top + sign * pltpu.roll(low, half, 1)
-                    cross[pl.ds(base + b, 16, stride=stride_k), :] = value
-        at = pl.multiple_of(step * count_k, LANE)
-        for q in range(16):
-            turned = cross[q * stride_k : q * stride_k + count_k, :].astype(BF16).T
-            stacked[q * half : (q + 1) * half, pl.ds(at, count_k)] = turned[:half]
-            stacked[q * half : (q + 1) * half, pl.ds(BINS + at, count_k)] = turned[half:]
-
-    @pl.when(step >= CHUNKS)
-    def _():
-        for r in range(1):
-            value = dot(stacked[...], lag_ref[...])
-            for q in range(16):
-                for side in range(2):
-                    spare[side, (q) * 72 : (q) * 72 + half, :] = value[
-                        q * half : (q + 1) * half, side * LANE : (side + 1) * LANE
-                    ]
-        for p in range(half):
-            for side in range(2):
-                out_ref[p * 16 : p * 16 + 16, side * LANE : (side + 1) * LANE] = spare[
-                    side, pl.ds(p, 16, stride=stride_p), :
-                ]
-
-
-def correlate(row_all, col_all):
-    segments = row_all.shape[0]
-    row_all = row_all.reshape(segments, QUARTERS, LANE, LANE)
-    table = lag_table()
+    at = pl.multiple_of(chunk * count_k, LANE)
+    for q in range(16):
+        turned = cross[q * STRIDE_K : q * STRIDE_K + count_k, :].astype(BF16).T
+        stacked[q * half : (q + 1) * half, pl.ds(at, count_k)] = turned[:half]
+        stacked[q * half : (q + 1) * half, pl.ds(BINS + at, count_k)] = turned[half:]
+
+
+def spectra(records, tile_blocks, live_len):
+    dma = pltpu.SemaphoreType.DMA
+    vmem = pl.BlockSpec(memory_space=pltpu.VMEM)
+    smem = pl.BlockSpec(memory_space=pltpu.SMEM)
+    return pl.pallas_call(
+        spectra_kernel,
+        in_specs=[smem, smem, vmem],
+        out_specs=vmem,
+        out_shape=jax.ShapeDtypeStruct((PAIRS, 2 * BINS), BF16),
+        scratch_shapes=[
+            pltpu.VMEM((LANE, LANE), BF16),
+            pltpu.VMEM((LANE, LANE), BF16),
+            pltpu.VMEM((5 * LANE, 2 * LANE), BF16),
+            pltpu.VMEM((2 * BINS, SEG), BF16),
+            pltpu.VMEM((2 * BINS, SEG), BF16),
+            pltpu.VMEM((BINS + 16, LANE), F32),
+            pltpu.VMEM((BINS, LANE), BF16),
+            pltpu.VMEM((4, LANE, LANE), BF16),
+            pltpu.VMEM((4 * RING, BINS, LANE), BF16),
+            pltpu.VMEM((4 * RING, LANE, LANE), BF16),
+            pltpu.VMEM((2 * RING, LANE, LANE), BF16),
+            pltpu.VMEM((4 * RING * STRIDE_K, LANE), F32),
+            pltpu.VMEM((4 * RING * STRIDE_C, LANE), F32),
+            pltpu.VMEM((16 * STRIDE_K, LANE), F32),
+            dma((2,)),
+            dma((3, 8, PARTS)), dma((32, PARTS)), dma((2, 8, PARTS)), dma((32, PARTS)),
+            dma((4,)), dma((2 * RING,)), dma((32, 2)), dma((32,)), dma((2 * RING + 1,)),
+        ],
+        compiler_params=pltpu.CompilerParams(
+            collective_id=0, has_side_effects=True, vmem_limit_bytes=48 << 20
+        ),
+        name="spectra",
+    )(tile_blocks, live_len, records)
+
+
+def lags_kernel(stacked, lag_ref, out_ref, spare):
+    half = LANE // 2
+    value = dot(stacked[...], lag_ref[...])
+    for q in range(16):
+        for side in range(2):
+            spare[side, q * STRIDE_P : q * STRIDE_P + half, :] = value[
+                q * half : (q + 1) * half, side * LANE : (side + 1) * LANE
+            ]
+    for p in range(half):
+        for side in range(2):
+            out_ref[p * 16 : p * 16 + 16, side * LANE : (side + 1) * LANE] = spare[
+                side, pl.ds(p, 16, stride=STRIDE_P), :
+            ]
+
+
+def lags(stacked):
     width = 2 * LANE
     tiles = -(-LAGS // width)
-    table = jnp.asarray(np.pad(table, ((0, 0), (0, tiles * width - LAGS))))
-    pairs = 16 * (LANE // 2)
-
-    body = functools.partial(correlate_kernel, segments)
+    table = jnp.asarray(np.pad(lag_table(), ((0, 0), (0, tiles * width - LAGS))))
     return pl.pallas_call(
-        body,
-        grid=(CHUNKS + tiles,),
+        lags_kernel,
+        grid=(tiles,),
         in_specs=[
-            pl.BlockSpec(
-                (segments, QUARTERS, KCHUNK, LANE),
-                lambda i: (0, 0, jnp.minimum(i, CHUNKS - 1), 0),
-            ),
-            pl.BlockSpec(
-                (segments, KCHUNK, LANE), lambda i: (0, jnp.minimum(i, CHUNKS - 1), 0)
-            ),
-            pl.BlockSpec((2 * BINS, width), lambda i: (0, jnp.maximum(i - CHUNKS, 0))),
+            pl.BlockSpec((PAIRS, 2 * BINS), lambda i: (0, 0)),
+            pl.BlockSpec((2 * BINS, width), lambda i: (0, i)),
         ],
-        out_specs=pl.BlockSpec((pairs, width), lambda i: (0, jnp.maximum(i - CHUNKS, 0))),
-        out_shape=jax.ShapeDtypeStruct((pairs, LAGS), F32),
-        scratch_shapes=[
-            pltpu.VMEM((segments * (QUARTERS * KCHUNK + 8), LANE), F32),
-            pltpu.VMEM((segments * (KCHUNK + 8), LANE), F32),
-            pltpu.VMEM((16 * (QUARTERS * KCHUNK + 8), LANE), F32),
-            pltpu.VMEM((pairs, 2 * BINS), BF16),
-            pltpu.VMEM((2, 16 * 72, LANE), F32),
-        ],
-        compiler_params=pltpu.CompilerParams(vmem_limit_bytes=48 << 20),
-        name="correlate",
-    )(row_all, col_all, table)
+        out_specs=pl.BlockSpec((PAIRS, width), lambda i: (0, i)),
+        out_shape=jax.ShapeDtypeStruct((PAIRS, LAGS), F32),
+        scratch_shapes=[pltpu.VMEM((2, 16 * STRIDE_P, LANE), F32)],
+        compiler_params=pltpu.CompilerParams(vmem_limit_bytes=32 << 20),
+        name="lags",
+    )(stacked, table)
 
 
 def shards(records, tile_blocks, live_len):
-    length = records.shape[2]
-    size = lax.axis_size("tm")
-    tails = lax.ppermute(
-        records[:, :, length - LANE :], "tm", [(i, i + 1) for i in range(size - 1)]
-    )
-    row_own, col_own = prepare(records, tails, tile_blocks, live_len)
-    row_all, col_all = exchange(row_own, col_own)
-    result = correlate(row_all, col_all)
+    result = lags(spectra(records, tile_blocks, live_len))
     return result.reshape(LANE // 2, 16, LAGS)
 
 

time: 79.1 us -> 66.6 us (0.84)
  waiting for transfers between devices: 8.06 us -> 0 us
  local copies, waits for them, and re-layouts: 5.9 us -> 2.69 us
  starting transfers between devices: 1.91 us -> 0 us
  Pallas kernels: 62.9 us -> 63.8 us
    ppermute x1 -> x0, waiting for transfers between devices: 8.06 us -> none  [shards(): lax.ppermute(records[:, :, length - LANE:], 'tm', [(i, i + 1) for i in ra...]
    unnamed x14 -> x8, local copies, waits for them, and re-layouts: 5.06 us -> 2.69 us
    ppermute x1 -> x0, starting transfers between devices: 1.91 us -> none  [shards(): lax.ppermute(records[:, :, length - LANE:], 'tm', [(i, i + 1) for i in ra...]
    pallas_call x3 -> x2, Pallas kernels: 62.9 us -> 63.8 us  [the longest x1 59.4 us: spectra(): pl.pallas_call(spectra_kernel, in_specs=[smem, smem, vmem], out_specs=vme...]
    slice x1 -> x0, local copies, waits for them, and re-layouts: 0.84 us -> none  [shards(): records[:, :, length - LANE:]]
  transfers between devices with their start and end apart: 1 -> 0, of which waited for: 1 -> 0; matrix products, arithmetic and copies ran while one was open for 0% -> 0% of each run, Pallas kernels for 0% -> 0%
where the time goes in v4:
time: 66.6 us; the launch traced here: 66.5 us
  Pallas kernels  63.8 us (96%)
  local copies, waits for them, and re-layouts  2.69 us (4%)
    pallas_call x1, Pallas kernels, spectra(): pl.pallas_call(spectra_kernel, in_specs=[smem, smem, vmem], out_specs=vme...  59.4 us
    pallas_call x1, Pallas kernels, lags(): pl.pallas_call(lags_kernel, grid=(tiles,), in_specs=[pl.BlockSpec((PAIRS,...  4.41 us
    unnamed x8, local copies, waits for them, and re-layouts  2.69 us

profile of v4, /device:TPU:14, one launch (start us, length us, event | category | flops | bytes accessed | tf_op | source)
XLA Modules:
  0.0 66.5 jit_solution(14225976272967963631)
XLA Ops:
  0.0 0.0 copy-start
  0.0 0.0 copy-start.1
  0.0 1.4 %copy-done.1 = bf16[4,64,2048]{2,1,0:T(8,128)(2,1)S(1)} copy-done((bf16[4,64,2048]{2,1,0:T(8,128)(2,1)S(1)}, bf16[4,64,2048]{2,1,0:T(8,128)(2,1)}, u32[]{:S(2)}) %copy-start.1) | copy-done | bytes 1048600
  1.4 0.0 copy-start.2
  1.4 0.7 copy-done.2
  2.0 0.0 copy-start.3
  2.0 0.7 copy-done.3
  2.7 59.4 %spectra.1.stacked = bf16[1024,1024]{1,0:T(8,128)(2,1)S(1)} custom-call(s32[2]{0:T(128)S(1)} %copy-done.2, s32[32]{0:T(128)S(1)} %copy-done.3, bf16[4,64,2048]{2,1,0:T(8,128)(2,1)S(1)} %copy-done.1), custom_call_target="tpu_custom_call" | custom-call | tf_op jit(solution)/shard_map/spectra/pallas_call | solution.py:525
  62.1 0.0 copy-done
  62.1 4.4 %lags.1 = f32[1024,801]{1,0:T(8,128)} custom-call(bf16[1024,1024]{1,0:T(8,128)(2,1)S(1)} %spectra.1.stacked, bf16[1024,1024]{1,0:T(8,128)(2,1)S(1)} %copy-done), custom_call_target="tpu_custom_call" | custom-call | tf_op jit(solution)/shard_map/lags/pallas_call | solution.py:575
Async XLA Ops:
  0.0 62.1 %copy-start = (bf16[1024,1024]{1,0:T(8,128)(2,1)S(1)}, bf16[1024,1024]{1,0:T(8,128)(2,1)}, u32[]{:S(2)}) copy-start(bf16[1024,1024]{1,0:T(8,128)(2,1)} %constant.2.clone.lag_ref) | copy-start | bytes 6291460
  0.0 1.4 %copy-start.1 = (bf16[4,64,2048]{2,1,0:T(8,128)(2,1)S(1)}, bf16[4,64,2048]{2,1,0:T(8,128)(2,1)}, u32[]{:S(2)}) copy-start(bf16[4,64,2048]{2,1,0:T(8,128)(2,1)} %records.1) | copy-start | bytes 3145732
  1.4 0.7 copy-start.2
  2.0 0.7 copy-start.3

commit v5 on v4

--- a/solution.py
+++ b/solution.py
@@ -34,7 +34,7 @@
 OFFSETS = (0, 1, -1, 2, -2, 3, -3, 4)
 PARTS = 2
 OPP_TIME = 3.0
-ROW_START, ROW_STEP = 5.0, 5.0
+ROW_START, ROW_STEP = 6.0, 6.0
 COL_STEP = 1.5
 COL_TIMES = (
     ("root", 1.5),
@@ -200,10 +200,10 @@
 
 
 def spectra_kernel(
-    blocks, live, records, stacked,
-    tail_own, tail_in, taps_ref, fwd_high, fwd_low, padded, row_ref, col_ref,
+    blocks_in, live_in, records_in, stacked_out,
+    stacked, blocks, live, records, tail_own, tail_in, taps_ref, fwd_high, fwd_low, padded, row_ref, col_ref,
     row_all, col_all, stage, rows, cols, cross,
-    tail_sem, row_send, row_recv, near_send, near_recv, stage_send, stage_recv,
+    out_sem, load_sem, tail_sem, row_send, row_recv, near_send, near_recv, stage_send, stage_recv,
     col_send, col_recv, local_sem,
 ):
     me = Place()
@@ -220,6 +220,14 @@
     up, down = lax.rem(me.y + 1, YRING), lax.rem(me.y + YRING - 1, YRING)
     right, left = lax.rem(me.z + 1, RING), lax.rem(me.z + RING - 1, RING)
 
+    loads = [
+        pltpu.make_async_copy(source, target, load_sem.at[i])
+        for i, (source, target) in enumerate(
+            ((records_in, records), (blocks_in, blocks), (live_in, live))
+        )
+    ]
+    for load in loads:
+        load.start()
     barrier = pltpu.get_barrier_semaphore()
 
     def greet(device):
@@ -242,7 +250,8 @@
         )
 
     fill_taps(taps_ref)
-    fill_transform(fwd_high, fwd_low)
+    for load in loads:
+        load.wait()
     length = records.shape[2]
     stations = records.shape[1]
     for side in range(2):
@@ -258,6 +267,7 @@
         {"pair": lax.axis_index("pair"), "tm": after},
     )
     pl.when(tm < 4 * RING - 1)(tail_copy.start)
+    fill_transform(fwd_high, fwd_low)
     count = live[tm]
     lane = lax.broadcasted_iota(jnp.int32, (1, LANE), 1)
     record = jnp.concatenate([records[blocks[0]], records[blocks[1]]], axis=0)
@@ -459,9 +469,26 @@
             pl.when(when)(copy.wait_send)
     pl.when(tm < 4 * RING - 1)(tail_copy.wait_send)
 
+    def chunk_copies(chunk):
+        return [
+            pltpu.make_async_copy(
+                stacked.at[:, pl.ds(pl.multiple_of(side * BINS + chunk * LANE, LANE), LANE)],
+                stacked_out.at[:, pl.ds(pl.multiple_of(side * BINS + chunk * LANE, LANE), LANE)],
+                out_sem.at[side, chunk],
+            )
+            for side in range(2)
+        ]
+
     @pl.loop(0, CHUNKS)
     def _(chunk):
         cross_chunk(chunk, row_all, col_all, rows, cols, cross, stacked)
+        for copy in chunk_copies(chunk):
+            copy.start()
+
+    @pl.loop(0, CHUNKS)
+    def _(chunk):
+        for copy in chunk_copies(chunk):
+            copy.wait()
 
 
 def cross_chunk(chunk, row_all, col_all, rows, cols, cross, stacked):
@@ -520,14 +547,16 @@
 
 def spectra(records, tile_blocks, live_len):
     dma = pltpu.SemaphoreType.DMA
-    vmem = pl.BlockSpec(memory_space=pltpu.VMEM)
-    smem = pl.BlockSpec(memory_space=pltpu.SMEM)
     return pl.pallas_call(
         spectra_kernel,
-        in_specs=[smem, smem, vmem],
-        out_specs=vmem,
+        in_specs=[pl.BlockSpec(memory_space=pltpu.HBM)] * 3,
+        out_specs=pl.BlockSpec(memory_space=pltpu.HBM),
         out_shape=jax.ShapeDtypeStruct((PAIRS, 2 * BINS), BF16),
         scratch_shapes=[
+            pltpu.VMEM((PAIRS, 2 * BINS), BF16),
+            pltpu.SMEM(tile_blocks.shape, jnp.int32),
+            pltpu.SMEM(live_len.shape, jnp.int32),
+            pltpu.VMEM(records.shape, BF16),
             pltpu.VMEM((LANE, LANE), BF16),
             pltpu.VMEM((LANE, LANE), BF16),
             pltpu.VMEM((5 * LANE, 2 * LANE), BF16),
@@ -542,12 +571,12 @@
             pltpu.VMEM((4 * RING * STRIDE_K, LANE), F32),
             pltpu.VMEM((4 * RING * STRIDE_C, LANE), F32),
             pltpu.VMEM((16 * STRIDE_K, LANE), F32),
-            dma((2,)),
+            dma((2, CHUNKS)), dma((3,)), dma((2,)),
             dma((3, 8, PARTS)), dma((32, PARTS)), dma((2, 8, PARTS)), dma((32, PARTS)),
             dma((4,)), dma((2 * RING,)), dma((32, 2)), dma((32,)), dma((2 * RING + 1,)),
         ],
         compiler_params=pltpu.CompilerParams(
-            collective_id=0, has_side_effects=True, vmem_limit_bytes=48 << 20
+            collective_id=0, has_side_effects=True, vmem_limit_bytes=60 << 20
         ),
         name="spectra",
     )(tile_blocks, live_len, records)

time: 66.6 us -> 62.7 us (0.941)
  Pallas kernels: 63.8 us -> 61 us
  local copies, waits for them, and re-layouts: 2.69 us -> 1.59 us
    pallas_call x1, Pallas kernels: 59.4 us -> 56.6 us  [spectra(): pl.pallas_call(spectra_kernel, in_specs=[pl.BlockSpec(memory_space=pltpu....]
    unnamed x8 -> x4, local copies, waits for them, and re-layouts: 2.69 us -> 1.59 us
where the time goes in v5:
time: 62.7 us; the launch traced here: 62.6 us
  Pallas kernels  61 us (97%)
  local copies, waits for them, and re-layouts  1.59 us (3%)
    pallas_call x1, Pallas kernels, spectra(): pl.pallas_call(spectra_kernel, in_specs=[pl.BlockSpec(memory_space=pltpu....  56.6 us
    pallas_call x1, Pallas kernels, lags(): pl.pallas_call(lags_kernel, grid=(tiles,), in_specs=[pl.BlockSpec((PAIRS,...  4.38 us
    unnamed x4, local copies, waits for them, and re-layouts  1.59 us

profile of v5, /device:TPU:14, one launch (start us, length us, event | category | flops | bytes accessed | tf_op | source)
XLA Modules:
  0.0 62.6 jit_solution(15146427082674007428)
XLA Ops:
  0.0 0.0 copy-start.1
  0.0 56.6 %spectra.1.stacked = bf16[1024,1024]{1,0:T(8,128)(2,1)} custom-call(s32[2]{0:T(128)} %blocks_in.1, s32[32]{0:T(128)} %live_in.1, bf16[4,64,2048]{2,1,0:T(8,128)(2,1)} %records_in.1), custom_call_target="tpu_custom_call" | custom-call | tf_op jit(solution)/shard_map/spectra/pallas_call | solution.py:550
  56.7 0.0 copy-done.1
  56.7 0.0 copy-start
  56.7 1.6 %copy-done = bf16[1024,1024]{1,0:T(8,128)(2,1)S(1)} copy-done((bf16[1024,1024]{1,0:T(8,128)(2,1)S(1)}, bf16[1024,1024]{1,0:T(8,128)(2,1)}, u32[]{:S(2)}) %copy-start) | copy-done | bytes 2097176
  58.3 4.4 %lags.1 = f32[1024,801]{1,0:T(8,128)} custom-call(bf16[1024,1024]{1,0:T(8,128)(2,1)S(1)} %copy-done, bf16[1024,1024]{1,0:T(8,128)(2,1)S(1)} %copy-done.1), custom_call_target="tpu_custom_call" | custom-call | tf_op jit(solution)/shard_map/lags/pallas_call | solution.py:604
Async XLA Ops:
  0.0 56.7 %copy-start.1 = (bf16[1024,1024]{1,0:T(8,128)(2,1)S(1)}, bf16[1024,1024]{1,0:T(8,128)(2,1)}, u32[]{:S(2)}) copy-start(bf16[1024,1024]{1,0:T(8,128)(2,1)} %constant.2.clone.lag_ref) | copy-start | bytes 6291460
  56.7 1.6 %copy-start = (bf16[1024,1024]{1,0:T(8,128)(2,1)S(1)}, bf16[1024,1024]{1,0:T(8,128)(2,1)}, u32[]{:S(2)}) copy-start(bf16[1024,1024]{1,0:T(8,128)(2,1)} %spectra.1.stacked) | copy-start | bytes 6291460

commit v6 on v5

--- a/solution.py
+++ b/solution.py
@@ -39,9 +39,9 @@
 COL_TIMES = (
     ("root", 1.5),
     ("other", 8.0),
-    ("near", 10.5),
-    ("hop1", 13.0),
-    ("hop2", 16.0),
+    ("near", 8.1),
+    ("hop1", 11.0),
+    ("hop2", 14.0),
     ("last", 40.0),
 )
 
@@ -320,7 +320,6 @@
 
     pack_rows(real, imag, row_ref)
     own = slot_of(me.xh, me.c, me.z)
-    own_local = pltpu.make_async_copy(row_ref, row_all.at[own], local_sem.at[2 * RING])
 
     def part(s):
         return pl.ds(s * size, size)
@@ -349,6 +348,10 @@
         ref = row_all.at[slot, part(s)]
         remote(ref, ref, row_send.at[0, 0, 0], sems.at[slot, s], me.at()).wait_recv()
 
+    def widen_part(slot, s):
+        each = QUARTERS // PARTS
+        widen(row_all.at[slot], slot, range(s * each, (s + 1) * each), rows)
+
     def got_col(slot):
         ref = col_all.at[slot]
         remote(ref, ref, col_send.at[0, 0], col_recv.at[slot], me.at()).wait_recv()
@@ -362,7 +365,7 @@
         )
     for s in range(PARTS):
         spread(row_ref, own, 0, 0, 0, s)
-    own_local.start()
+    widen(row_ref, own, range(QUARTERS), rows)
 
     def zpiece(i):
         return lax.rem(me.z + OFFSETS[i] + RING, RING)
@@ -394,6 +397,7 @@
             slot = slot_of(1 - me.xh, me.c, me.z)
             got_row(slot, arg, row_recv)
             spread(row_all.at[slot], slot, 1, 0, 0, arg)
+            widen_part(slot, arg)
         elif kind == "row":
             h, d, s = arg
             xh = me.xh if h == 0 else 1 - me.xh
@@ -402,6 +406,7 @@
                 slot = slot_of(xh, me.c, lax.rem(me.z - sign * d + RING, RING))
                 got_row(slot, s, row_recv)
                 spread(row_all.at[slot], slot, h, d, sign, s)
+                widen_part(slot, s)
         elif kind == "root":
             for c in range(2):
                 index = c * RING + zpiece(arg)
@@ -421,13 +426,17 @@
 
                 sideways(stage.at[index], slot, is_near)
                 sideways(stage.at[index], slot, is_far, xh=1 - me.xh)
+                start(
+                    remote(
+                        stage.at[index], col_all.at[slot], col_send.at[slot, 2],
+                        col_recv.at[slot], me.at(xh=1 - me.xh),
+                    ),
+                    is_far,
+                )
                 along(stage.at[index], slot, c, is_near)
         elif kind == "other":
             for c in range(2):
-                slot = slot_of(1 - me.xh, c, zpiece(arg))
-                pl.when(is_other)(lambda slot=slot: got_col(slot))
-                sideways(col_all.at[slot], slot, is_other)
-                along(col_all.at[slot], slot, c, is_other)
+                hop(slot_of(1 - me.xh, c, zpiece(arg)), c, is_other)
             for c in range(2):
                 hop(slot_of(me.xh, c, zpiece(arg)), c, is_other)
         elif kind == "near":
@@ -449,8 +458,9 @@
     for h in range(2):
         for z in range(RING):
             for s in range(PARTS):
-                got_row(slot_of(h, 1 - me.c, z), s, near_recv)
-    own_local.wait()
+                slot = slot_of(h, 1 - me.c, z)
+                got_row(slot, s, near_recv)
+                widen_part(slot, s)
     for i in range(RING):
         for c in range(2):
             index = c * RING + zpiece(i)
@@ -491,6 +501,16 @@
             copy.wait()
 
 
+def widen(source, slot, quarters, rows):
+    for chunk in range(CHUNKS):
+        for quarter in quarters:
+            at = (chunk * (4 * RING) + slot) * STRIDE_K + quarter * KCHUNK
+            first = quarter * LANE + chunk * KCHUNK
+            rows[pl.ds(pl.multiple_of(at, 8), KCHUNK), :] = source[
+                first : first + KCHUNK, :
+            ].astype(F32)
+
+
 def cross_chunk(chunk, row_all, col_all, rows, cols, cross, stacked):
     segments = row_all.shape[0]
     half = LANE // 2
@@ -498,11 +518,6 @@
     count_k = QUARTERS * KCHUNK
     first = pl.multiple_of(chunk * KCHUNK, KCHUNK)
     for g in range(segments):
-        for quarter in range(QUARTERS):
-            at = g * STRIDE_K + quarter * KCHUNK
-            rows[at : at + KCHUNK, :] = row_all[
-                g, pl.ds(quarter * LANE + first, KCHUNK), :
-            ].astype(F32)
         cols[g * STRIDE_C : g * STRIDE_C + KCHUNK, :] = col_all[
             g, pl.ds(first, KCHUNK), :
         ].astype(F32)
@@ -528,7 +543,7 @@
             )
             base = quarter * KCHUNK + block * group
             right = jnp.concatenate(
-                [rows[pl.ds(base + b, segments, stride=STRIDE_K), :] for b in range(group)],
+                [rows[pl.ds(chunk * (segments * STRIDE_K) + base + b, segments, stride=STRIDE_K), :] for b in range(group)],
                 axis=0,
             ).astype(BF16)
             product = dot(wide, right)
@@ -568,12 +583,12 @@
             pltpu.VMEM((4 * RING, BINS, LANE), BF16),
             pltpu.VMEM((4 * RING, LANE, LANE), BF16),
             pltpu.VMEM((2 * RING, LANE, LANE), BF16),
-            pltpu.VMEM((4 * RING * STRIDE_K, LANE), F32),
+            pltpu.VMEM((CHUNKS * 4 * RING * STRIDE_K, LANE), F32),
             pltpu.VMEM((4 * RING * STRIDE_C, LANE), F32),
             pltpu.VMEM((16 * STRIDE_K, LANE), F32),
             dma((2, CHUNKS)), dma((3,)), dma((2,)),
             dma((3, 8, PARTS)), dma((32, PARTS)), dma((2, 8, PARTS)), dma((32, PARTS)),
-            dma((4,)), dma((2 * RING,)), dma((32, 2)), dma((32,)), dma((2 * RING + 1,)),
+            dma((4,)), dma((2 * RING,)), dma((32, 3)), dma((32,)), dma((2 * RING + 1,)),
         ],
         compiler_params=pltpu.CompilerParams(
             collective_id=0, has_side_effects=True, vmem_limit_bytes=60 << 20

time: 62.7 us -> 60.8 us (0.970)
  Pallas kernels: 61 us -> 59.1 us
    pallas_call x1, Pallas kernels: 56.6 us -> 54.7 us  [spectra(): pl.pallas_call(spectra_kernel, in_specs=[pl.BlockSpec(memory_space=pltpu....]
where the time goes in v6:
time: 60.8 us; the launch traced here: 60.7 us
  Pallas kernels  59.1 us (97%)
  local copies, waits for them, and re-layouts  1.59 us (3%)
    pallas_call x1, Pallas kernels, spectra(): pl.pallas_call(spectra_kernel, in_specs=[pl.BlockSpec(memory_space=pltpu....  54.7 us
    pallas_call x1, Pallas kernels, lags(): pl.pallas_call(lags_kernel, grid=(tiles,), in_specs=[pl.BlockSpec((PAIRS,...  4.38 us
    unnamed x4, local copies, waits for them, and re-layouts  1.59 us

profile of v6, /device:TPU:14, one launch (start us, length us, event | category | flops | bytes accessed | tf_op | source)
XLA Modules:
  0.0 60.7 jit_solution(8375992669650013145)
XLA Ops:
  0.0 0.0 copy-start.1
  0.0 54.7 %spectra.1.stacked = bf16[1024,1024]{1,0:T(8,128)(2,1)} custom-call(s32[2]{0:T(128)} %blocks_in.1, s32[32]{0:T(128)} %live_in.1, bf16[4,64,2048]{2,1,0:T(8,128)(2,1)} %records_in.1), custom_call_target="tpu_custom_call" | custom-call | tf_op jit(solution)/shard_map/spectra/pallas_call | solution.py:565
  54.7 0.0 copy-done.1
  54.7 0.0 copy-start
  54.7 1.6 %copy-done = bf16[1024,1024]{1,0:T(8,128)(2,1)S(1)} copy-done((bf16[1024,1024]{1,0:T(8,128)(2,1)S(1)}, bf16[1024,1024]{1,0:T(8,128)(2,1)}, u32[]{:S(2)}) %copy-start) | copy-done | bytes 2097176
  56.3 4.4 %lags.1 = f32[1024,801]{1,0:T(8,128)} custom-call(bf16[1024,1024]{1,0:T(8,128)(2,1)S(1)} %copy-done, bf16[1024,1024]{1,0:T(8,128)(2,1)S(1)} %copy-done.1), custom_call_target="tpu_custom_call" | custom-call | tf_op jit(solution)/shard_map/lags/pallas_call | solution.py:619
Async XLA Ops:
  0.0 54.7 %copy-start.1 = (bf16[1024,1024]{1,0:T(8,128)(2,1)S(1)}, bf16[1024,1024]{1,0:T(8,128)(2,1)}, u32[]{:S(2)}) copy-start(bf16[1024,1024]{1,0:T(8,128)(2,1)} %constant.2.clone.lag_ref) | copy-start | bytes 6291460
  54.7 1.6 %copy-start = (bf16[1024,1024]{1,0:T(8,128)(2,1)S(1)}, bf16[1024,1024]{1,0:T(8,128)(2,1)}, u32[]{:S(2)}) copy-start(bf16[1024,1024]{1,0:T(8,128)(2,1)} %spectra.1.stacked) | copy-start | bytes 6291460

commit v7 on v6

--- a/solution.py
+++ b/solution.py
@@ -32,9 +32,9 @@
 RING = 8
 YRING = 4
 OFFSETS = (0, 1, -1, 2, -2, 3, -3, 4)
-PARTS = 2
+PARTS = 1
 OPP_TIME = 3.0
-ROW_START, ROW_STEP = 6.0, 6.0
+ROW_START, ROW_STEP = 6.5, 6.5
 COL_STEP = 1.5
 COL_TIMES = (
     ("root", 1.5),
@@ -325,7 +325,7 @@
         return pl.ds(s * size, size)
 
     def spread(source, slot, h, d, sign, s):
-        lower = s < PARTS // 2
+        lower = h == 0
         for way, target in ((1, right), (-1, left)):
             if sign not in (0, way) or d > 3 or (d == 3 and lower != (way == 1)):
                 continue
@@ -401,7 +401,7 @@
         elif kind == "row":
             h, d, s = arg
             xh = me.xh if h == 0 else 1 - me.xh
-            signs = (1, -1) if d < 4 else ((1,) if s < PARTS // 2 else (-1,))
+            signs = (1, -1) if d < 4 else ((1,) if h == 0 else (-1,))
             for sign in signs:
                 slot = slot_of(xh, me.c, lax.rem(me.z - sign * d + RING, RING))
                 got_row(slot, s, row_recv)

time: 60.8 us -> 60.2 us (level)
  Pallas kernels: 59.1 us -> 57.9 us
    pallas_call x1, Pallas kernels: 54.7 us -> 53.5 us  [spectra(): pl.pallas_call(spectra_kernel, in_specs=[pl.BlockSpec(memory_space=pltpu....]
where the time goes in v7:
time: 60.2 us; the launch traced here: 59.5 us
  Pallas kernels  57.9 us (96%)
  local copies, waits for them, and re-layouts  1.59 us (3%)
    pallas_call x1, Pallas kernels, spectra(): pl.pallas_call(spectra_kernel, in_specs=[pl.BlockSpec(memory_space=pltpu....  53.5 us
    pallas_call x1, Pallas kernels, lags(): pl.pallas_call(lags_kernel, grid=(tiles,), in_specs=[pl.BlockSpec((PAIRS,...  4.38 us
    unnamed x4, local copies, waits for them, and re-layouts  1.59 us

profile of v7, /device:TPU:14, one launch (start us, length us, event | category | flops | bytes accessed | tf_op | source)
XLA Modules:
  0.0 59.5 jit_solution(266556315286538589)
XLA Ops:
  0.0 0.0 copy-start.1
  0.0 53.5 %spectra.1.stacked = bf16[1024,1024]{1,0:T(8,128)(2,1)} custom-call(s32[2]{0:T(128)} %blocks_in.1, s32[32]{0:T(128)} %live_in.1, bf16[4,64,2048]{2,1,0:T(8,128)(2,1)} %records_in.1), custom_call_target="tpu_custom_call" | custom-call | tf_op jit(solution)/shard_map/spectra/pallas_call | solution.py:565
  53.5 0.0 copy-done.1
  53.5 0.0 copy-start
  53.5 1.6 %copy-done = bf16[1024,1024]{1,0:T(8,128)(2,1)S(1)} copy-done((bf16[1024,1024]{1,0:T(8,128)(2,1)S(1)}, bf16[1024,1024]{1,0:T(8,128)(2,1)}, u32[]{:S(2)}) %copy-start) | copy-done | bytes 2097176
  55.1 4.4 %lags.1 = f32[1024,801]{1,0:T(8,128)} custom-call(bf16[1024,1024]{1,0:T(8,128)(2,1)S(1)} %copy-done, bf16[1024,1024]{1,0:T(8,128)(2,1)S(1)} %copy-done.1), custom_call_target="tpu_custom_call" | custom-call | tf_op jit(solution)/shard_map/lags/pallas_call | solution.py:619
Async XLA Ops:
  0.0 53.5 %copy-start.1 = (bf16[1024,1024]{1,0:T(8,128)(2,1)S(1)}, bf16[1024,1024]{1,0:T(8,128)(2,1)}, u32[]{:S(2)}) copy-start(bf16[1024,1024]{1,0:T(8,128)(2,1)} %constant.2.clone.lag_ref) | copy-start | bytes 6291460
  53.5 1.6 %copy-start = (bf16[1024,1024]{1,0:T(8,128)(2,1)S(1)}, bf16[1024,1024]{1,0:T(8,128)(2,1)}, u32[]{:S(2)}) copy-start(bf16[1024,1024]{1,0:T(8,128)(2,1)} %spectra.1.stacked) | copy-start | bytes 6291460

commit v8 on v7

--- a/solution.py
+++ b/solution.py
@@ -599,17 +599,23 @@
 
 def lags_kernel(stacked, lag_ref, out_ref, spare):
     half = LANE // 2
-    value = dot(stacked[...], lag_ref[...])
-    for q in range(16):
-        for side in range(2):
-            spare[side, q * STRIDE_P : q * STRIDE_P + half, :] = value[
-                q * half : (q + 1) * half, side * LANE : (side + 1) * LANE
-            ]
-    for p in range(half):
-        for side in range(2):
-            out_ref[p * 16 : p * 16 + 16, side * LANE : (side + 1) * LANE] = spare[
-                side, pl.ds(p, 16, stride=STRIDE_P), :
-            ]
+    full = LAGS // (2 * LANE)
+
+    def tile(sides):
+        value = dot(stacked[...], lag_ref[:, : sides * LANE])
+        for q in range(16):
+            for side in range(sides):
+                spare[side, q * STRIDE_P : q * STRIDE_P + half, :] = value[
+                    q * half : (q + 1) * half, side * LANE : (side + 1) * LANE
+                ]
+        for p in range(half):
+            for side in range(sides):
+                out_ref[p * 16 : p * 16 + 16, side * LANE : (side + 1) * LANE] = spare[
+                    side, pl.ds(p, 16, stride=STRIDE_P), :
+                ]
+
+    pl.when(pl.program_id(0) < full)(lambda: tile(2))
+    pl.when(pl.program_id(0) == full)(lambda: tile(1))
 
 
 def lags(stacked):

time: 60.2 us -> 60.1 us (level)
  no operation moved by 1% of the time
where the time goes in v8:
time: 60.1 us; the launch traced here: 59.5 us
  Pallas kernels  57.9 us (96%)
  local copies, waits for them, and re-layouts  1.59 us (3%)
    pallas_call x1, Pallas kernels, spectra(): pl.pallas_call(spectra_kernel, in_specs=[pl.BlockSpec(memory_space=pltpu....  53.5 us
    pallas_call x1, Pallas kernels, lags(): pl.pallas_call(lags_kernel, grid=(tiles,), in_specs=[pl.BlockSpec((PAIRS,...  4.36 us
    unnamed x4, local copies, waits for them, and re-layouts  1.59 us

profile of v8, /device:TPU:14, one launch (start us, length us, event | category | flops | bytes accessed | tf_op | source)
XLA Modules:
  0.0 59.5 jit_solution(14496766695218796408)
XLA Ops:
  0.0 0.0 copy-start.1
  0.0 53.5 %spectra.1.stacked = bf16[1024,1024]{1,0:T(8,128)(2,1)} custom-call(s32[2]{0:T(128)} %blocks_in.1, s32[32]{0:T(128)} %live_in.1, bf16[4,64,2048]{2,1,0:T(8,128)(2,1)} %records_in.1), custom_call_target="tpu_custom_call" | custom-call | tf_op jit(solution)/shard_map/spectra/pallas_call | solution.py:565
  53.5 0.0 copy-done.1
  53.5 0.0 copy-start
  53.5 1.6 %copy-done = bf16[1024,1024]{1,0:T(8,128)(2,1)S(1)} copy-done((bf16[1024,1024]{1,0:T(8,128)(2,1)S(1)}, bf16[1024,1024]{1,0:T(8,128)(2,1)}, u32[]{:S(2)}) %copy-start) | copy-done | bytes 2097176
  55.1 4.4 %lags.1 = f32[1024,801]{1,0:T(8,128)} custom-call(bf16[1024,1024]{1,0:T(8,128)(2,1)S(1)} %copy-done, bf16[1024,1024]{1,0:T(8,128)(2,1)S(1)} %copy-done.1), custom_call_target="tpu_custom_call" | custom-call | tf_op jit(solution)/shard_map/lags/pallas_call | solution.py:625
Async XLA Ops:
  0.0 53.5 %copy-start.1 = (bf16[1024,1024]{1,0:T(8,128)(2,1)S(1)}, bf16[1024,1024]{1,0:T(8,128)(2,1)}, u32[]{:S(2)}) copy-start(bf16[1024,1024]{1,0:T(8,128)(2,1)} %constant.2.clone.lag_ref) | copy-start | bytes 6291460
  53.5 1.6 %copy-start = (bf16[1024,1024]{1,0:T(8,128)(2,1)S(1)}, bf16[1024,1024]{1,0:T(8,128)(2,1)}, u32[]{:S(2)}) copy-start(bf16[1024,1024]{1,0:T(8,128)(2,1)} %spectra.1.stacked) | copy-start | bytes 6291460
